TPU v7x, 32 devices: a whole 2x2x4 slice. The times are simulated.
32 devices in a mesh: dp: 8 (over z, y), tp: 4 (over x, core).
Axes of the slice: x: 2, y: 2, z: 4, core: 2. Of those that a mesh axis runs over, the one named last changes fastest.
Arguments:
- tokens: bfloat16 [32, 1024, 768], P(('dp', 'tp')), may hold values from -11 to 11
- clip_lengths: int32 [32, 4], P(('dp', 'tp')), may hold values from 1 to 384, as said below
- out_grad: bfloat16 [32, 1024, 768], P(('dp', 'tp')), may hold values from -6 to 6
- w_query: bfloat16 [768, 768], P(('dp', 'tp')), may hold values from -0.21875 to 0.21875
- w_key: bfloat16 [768, 768], P(('dp', 'tp')), may hold values from -0.21875 to 0.21875
- w_value: bfloat16 [768, 768], P(('dp', 'tp')), may hold values from -0.21875 to 0.21875
- w_output: bfloat16 [768, 768], P(('dp', 'tp')), may hold values from -2.5 to 2.5
- gain_attention: bfloat16 [768], P(('dp', 'tp')), may hold values from 0.099609375 to 1.8984375
- gain_feed: bfloat16 [768], P(('dp', 'tp')), may hold values from 0.099609375 to 1.8984375
- w_expand: bfloat16 [768, 3072], P('dp', 'tp'), may hold values from -0.21875 to 0.21875
- w_reduce: bfloat16 [3072, 768], P('tp', 'dp'), may hold values from -0.4375 to 0.4375
Outputs:
- block_out: bfloat16 [32, 1024, 768], P(('dp', 'tp'))
- grad_tokens: float32 [32, 1024, 768], P(('dp', 'tp'))
- grad_w_query: float32 [768, 768], P(('dp', 'tp'))
- grad_w_key: float32 [768, 768], P(('dp', 'tp'))
- grad_w_value: float32 [768, 768], P(('dp', 'tp'))
- grad_w_output: float32 [768, 768], P(('dp', 'tp'))
- grad_gain_attention: float32 [768], P(('dp', 'tp'))
- grad_gain_feed: float32 [768], P(('dp', 'tp'))
- grad_w_expand: float32 [768, 3072], P('dp', 'tp')
- grad_w_reduce: float32 [3072, 768], P('tp', 'dp')
- root_mean_squares: float32 [3], replicated
Inputs may be any that keep to these rules, and one draw needn't show every extreme that they name: Each row of clip_lengths gives the lengths of its 3 clips in order, each at most 384 with one of exactly 384 in every row, then the number of padding slots at the row's end, 1 to 256; a row's entries sum to 1024.
All inputs are finite; a program needn't handle non-finite values.
Results may differ from a plain program's by a relative error of at most 0.015.
Values may be sent and summed in bfloat16 or wider, within the bound.
A program may use at most 192 MiB of HBM per device.

v0:
```python
import jax
import jax.numpy as jnp
import numpy as np
from jax import lax
from jax.experimental import pallas as pl
from jax.experimental.pallas import tpu as pltpu
from jax.sharding import PartitionSpec as P

HEADS = 12
HEAD_DIM = 64
SLOTS = 4
LANES = 128
BLOCK = 256
WIDE = 512
MAXCLIP = 384
GROUP = 256
NEG = -1e30
f32 = jnp.float32
bf16 = jnp.bfloat16
BOTH = ("dp", "tp")
VM = pl.BlockSpec(memory_space=pltpu.VMEM)
SM = pl.BlockSpec(memory_space=pltpu.SMEM)


def dot_plain(left, right):
    return jnp.dot(left, right, preferred_element_type=f32)


def dot_first(left, right):
    return lax.dot_general(left, right, (((0,), (0,)), ((), ())), preferred_element_type=f32)


def dot_last(left, right):
    return lax.dot_general(left, right, (((1,), (1,)), ((), ())), preferred_element_type=f32)


def unit_of(rows):
    centred = rows - jnp.mean(rows, axis=-1, keepdims=True)
    inv = lax.rsqrt(jnp.mean(centred * centred, axis=-1, keepdims=True) + 1e-06)
    return centred * inv, inv


def unit_back(grad, unit, inv, gain):
    scaled = grad * gain
    inner = (
        scaled
        - jnp.mean(scaled, axis=-1, keepdims=True)
        - unit * jnp.mean(scaled * unit, axis=-1, keepdims=True)
    )
    return inv * inner


def clip_ends(clip_ref):
    ends, total = [], jnp.int32(0)
    for j in range(SLOTS - 1):
        total = total + clip_ref[0, j]
        ends.append(total)
    return ends


def segment_of(position, ends):
    return sum((position >= e).astype(jnp.int32) for e in ends)


def valid_of(start, count, ends):
    position = start + lax.broadcasted_iota(jnp.int32, (count, 1), 0)
    return (position < ends[-1]).astype(f32)


def window_of(low, high, ends, total):
    start, stop = jnp.int32(0), jnp.int32(total)
    for e in ends:
        start = jnp.where(low >= e, e, start)
    for e in ends[::-1]:
        stop = jnp.where(high < e, e, stop)
    block = start // LANES
    return block, (stop + LANES - 1) // LANES - block


def by_width(block, count, total, run):
    most = total // LANES
    widths = [w for w in range(2, most + 1) if w != most - 1]
    before = 0
    for w in widths:

        @pl.when((count > before) & (count <= w))
        def _(w=w):
            run(pl.multiple_of(jnp.minimum(block, most - w) * LANES, LANES), w * LANES)

        before = w


def row_loop(total, size, body):
    def step(i, carry):
        body(pl.multiple_of(i * size, size))
        return carry

    lax.fori_loop(0, total // size, step, 0)


def head_masks(scale):
    lane = lax.broadcasted_iota(jnp.int32, (1, LANES), 1)
    low = lane < HEAD_DIM
    return lane, low, (jnp.where(low, scale, 0.0).astype(bf16), jnp.where(low, 0.0, scale).astype(bf16))


def set_bias(bias_ref, row_start, rows, col_start, cols, ends):
    row_seg = segment_of(row_start + lax.broadcasted_iota(jnp.int32, (rows, 1), 0), ends)
    col_seg = segment_of(col_start + lax.broadcasted_iota(jnp.int32, (1, cols), 1), ends)
    bias_ref[:, :cols] = jnp.where(row_seg == col_seg, 0.0, NEG)


def attend(qkv_ref, ends, mixed_ref, stat_ref, bias_ref):
    total, width = mixed_ref.shape
    lane, low, scaled = head_masks(0.125)

    def block(r0):
        rows = pl.ds(r0, BLOCK)

        def run(k0, cols):
            win = pl.ds(k0, cols)
            set_bias(bias_ref, r0, BLOCK, k0, cols, ends)

            def pair(p, carry):
                c = pl.multiple_of(p * LANES, LANES)
                at = pl.multiple_of(p // 2 * (3 * GROUP) + p % 2 * LANES, LANES)
                query = qkv_ref[rows, pl.ds(at, LANES)]
                keys = qkv_ref[win, pl.ds(at + GROUP, LANES)]
                values = qkv_ref[win, pl.ds(at + 2 * GROUP, LANES)]
                values = jnp.concatenate([values, jnp.ones_like(values)], axis=1)
                stats, outs = stat_ref[rows, :], []
                for h, mask in enumerate(scaled):
                    scores = dot_last(query * mask, keys) + bias_ref[:, :cols]
                    top = jnp.max(scores, axis=1, keepdims=True)
                    mixed = dot_plain(jnp.exp(scores - top).astype(bf16), values)
                    row_sum = mixed[:, LANES:]
                    outs.append(mixed[:, :LANES] / row_sum)
                    stats = jnp.where(lane == 2 * p + h, top + jnp.log(row_sum), stats)
                stat_ref[rows, :] = stats
                mixed_ref[rows, pl.ds(c, LANES)] = jnp.where(low, outs[0], outs[1]).astype(bf16)
                return carry

            lax.fori_loop(0, width // LANES, pair, 0)

        by_width(*window_of(r0, r0 + BLOCK - 1, ends, total), total, run)

    row_loop(total, BLOCK, block)


def inner_sums(grad_ref, mixed_ref, stat_ref):
    total, width = mixed_ref.shape
    lane, low, _ = head_masks(1.0)

    def block(r0):
        rows = pl.ds(r0, LANES)
        sums = jnp.zeros((LANES, LANES), f32)
        for p in range(width // LANES):
            cols = slice(p * LANES, (p + 1) * LANES)
            both = grad_ref[rows, cols].astype(f32) * mixed_ref[rows, cols].astype(f32)
            first = jnp.sum(jnp.where(low, both, 0.0), axis=1, keepdims=True)
            second = jnp.sum(jnp.where(low, 0.0, both), axis=1, keepdims=True)
            sums = jnp.where(lane == 2 * p, first, jnp.where(lane == 2 * p + 1, second, sums))
        stat_ref[rows, :] = sums

    row_loop(total, LANES, block)


def group_lanes(width, g):
    start = width + LANES + g * 3 * GROUP
    return slice(start, start + 3 * GROUP)


def set_row(ref, row, value):
    at = lax.broadcasted_iota(jnp.int32, ref.shape, 0) == row
    ref[...] += jnp.where(at, value, 0.0)


def forward_kernel(
    clip_ref, tokens_ref, weights_ref, gains_ref,
    qkv_ref, mixed_ref, lse_ref, middle_ref, feed_ref, normed_ref, sums_ref,
    stat_ref, bias_ref,
):
    total, width = tokens_ref.shape
    ends = clip_ends(clip_ref)
    sums_ref[...] = jnp.zeros_like(sums_ref)

    def norm(r0):
        rows = pl.ds(r0, BLOCK)
        x = tokens_ref[rows, :].astype(f32)
        normed_ref[rows, :] = (unit_of(x)[0] * gains_ref[0:1, :]).astype(bf16)
        set_row(sums_ref, 0, jnp.sum(x * x * valid_of(r0, BLOCK, ends), axis=0, keepdims=True))

    row_loop(total, BLOCK, norm)
    for g in range(width // GROUP):
        cols = slice(g * 3 * GROUP, (g + 1) * 3 * GROUP)
        qkv_ref[:, cols] = dot_plain(normed_ref[...], weights_ref[:, group_lanes(width, g)]).astype(bf16)
    attend(qkv_ref, ends, mixed_ref, stat_ref, bias_ref)
    lse_ref[...] = stat_ref[...].T[: lse_ref.shape[0]]
    middle_ref[...] = dot_plain(mixed_ref[...], weights_ref[:, :width])

    def second(r0):
        rows = pl.ds(r0, BLOCK)
        branch = middle_ref[rows, :]
        middle = tokens_ref[rows, :].astype(f32) + branch
        middle_ref[rows, :] = middle
        feed_ref[rows, :] = (unit_of(middle)[0] * gains_ref[1:2, :]).astype(bf16)
        set_row(sums_ref, 1, jnp.sum(branch * branch * valid_of(r0, BLOCK, ends), axis=0, keepdims=True))

    row_loop(total, BLOCK, second)


def feed_kernel(
    clip_ref, feed_ref, out_grad_ref, middle_ref, gains_ref, weights_ref,
    grads_ref, result_ref, grad_middle_ref, sums_ref,
    grad_ref, active_ref, hidden_ref, out_ref, back_ref,
):
    total, width = feed_ref.shape
    ends = clip_ends(clip_ref)
    step = pl.program_id(0)

    @pl.when(step == 0)
    def _():
        def mask(r0):
            rows = pl.ds(r0, BLOCK)
            grad_ref[rows, :] = (out_grad_ref[rows, :].astype(f32) * valid_of(r0, BLOCK, ends)).astype(bf16)

        row_loop(total, BLOCK, mask)
        out_ref[...] = jnp.zeros_like(out_ref)
        back_ref[...] = jnp.zeros_like(back_ref)
        sums_ref[...] = jnp.zeros_like(sums_ref)

    hid = weights_ref.shape[2] - width
    part = 256
    for n in range(hid // part):
        cols = slice(n * part, (n + 1) * part)
        late = slice(hid + n * part, hid + (n + 1) * part)
        hidden = dot_plain(feed_ref[...], weights_ref[0, :, cols])
        grad_active = dot_plain(grad_ref[...], weights_ref[0, :, late])
        share = 0.5 * (1.0 + lax.erf(hidden * 0.7071067811865476))
        active_ref[:, cols] = (hidden * share).astype(bf16)
        slope = share + hidden * (jnp.exp(-0.5 * hidden * hidden) * 0.3989422804014327)
        hidden_ref[:, cols] = (grad_active * slope).astype(bf16)
    expand, reduce = weights_ref[0, :, :hid], weights_ref[0, :, hid:]
    out_ref[...] += dot_last(active_ref[...], reduce)
    back_ref[...] += dot_last(hidden_ref[...], expand)
    grads_ref[0, :, :hid] = dot_first(feed_ref[...], hidden_ref[...]).astype(bf16)
    grads_ref[0, :, hid:] = dot_first(grad_ref[...], active_ref[...]).astype(bf16)

    @pl.when(step == pl.num_programs(0) - 1)
    def _():
        def finish(r0):
            rows = pl.ds(r0, BLOCK)
            valid = valid_of(r0, BLOCK, ends)
            middle, out, back = middle_ref[rows, :], out_ref[rows, :], back_ref[rows, :]
            result_ref[rows, :] = (middle + out).astype(bf16)
            unit, inv = unit_of(middle)
            grad_middle_ref[rows, :] = (
                grad_ref[rows, :].astype(f32) + unit_back(back, unit, inv, gains_ref[1:2, :])
            )
            set_row(sums_ref, 0, jnp.sum(out * out * valid, axis=0, keepdims=True))
            set_row(sums_ref, 1, jnp.sum(back * unit, axis=0, keepdims=True))

        row_loop(total, BLOCK, finish)


def static_windows(total):
    spans = []
    for r0 in range(0, total, WIDE):
        low = max(0, r0 - MAXCLIP + 1) // LANES * LANES
        high = min(total, -(-(r0 + WIDE + MAXCLIP - 1) // LANES) * LANES)
        spans.append((low, high))
    width = max(high - low for low, high in spans)
    return [min(low, total - width) for low, _ in spans], width


def start_of(starts, block):
    at = jnp.int32(starts[0])
    for i, s in enumerate(starts):
        at = jnp.where(block == i, s, at)
    return pl.multiple_of(at, LANES)


def pair_forward(g, block, pair, total, qkv_ref, ends, mixed_ref, stat_ref, bias_ref):
    starts, cols = static_windows(total)
    lane, low, scaled = head_masks(0.125)
    r0 = pl.multiple_of(block * WIDE, WIDE)
    k0 = start_of(starts, block)
    rows, win = pl.ds(r0, WIDE), pl.ds(k0, cols)

    @pl.when(pair == 0)
    def _():
        set_bias(bias_ref, r0, WIDE, k0, cols, ends)

    c = pl.multiple_of(pair * LANES, LANES)
    at = pl.multiple_of(g * 3 * GROUP + c, LANES)
    query = qkv_ref[rows, pl.ds(at, LANES)]
    keys = qkv_ref[win, pl.ds(at + GROUP, LANES)]
    values = qkv_ref[win, pl.ds(at + 2 * GROUP, LANES)]
    values = jnp.concatenate([values, jnp.ones_like(values)], axis=1)
    stats, outs = stat_ref[rows, :], []
    for h, mask in enumerate(scaled):
        scores = dot_last(query * mask, keys) + bias_ref[:, :cols]
        top = jnp.max(scores, axis=1, keepdims=True)
        mixed = dot_plain(jnp.exp(scores - top).astype(bf16), values)
        row_sum = mixed[:, LANES:]
        outs.append(mixed[:, :LANES] / row_sum)
        stats = jnp.where(lane == 4 * g + 2 * pair + h, top + jnp.log(row_sum), stats)
    stat_ref[rows, :] = stats
    mixed_ref[rows, pl.ds(pl.multiple_of(g * GROUP + c, LANES), LANES)] = jnp.where(low, outs[0], outs[1]).astype(bf16)


def pair_back(g, block, pair, total, qkv_ref, ends, grad_ref, lse_ref, inner_ref, dqkv_ref, bias_ref, dq_ref):
    starts, cols = static_windows(total)
    _, low, scaled = head_masks(0.125)
    _, _, plain = head_masks(1.0)
    r0 = pl.multiple_of(block * WIDE, WIDE)
    q0 = start_of(starts, block)
    rows, win = pl.ds(r0, WIDE), pl.ds(q0, cols)

    @pl.when(pair == 0)
    def _():
        set_bias(bias_ref, r0, WIDE, q0, cols, ends)

    c = pl.multiple_of(pair * LANES, LANES)
    at = pl.multiple_of(g * 3 * GROUP + c, LANES)
    keys = qkv_ref[rows, pl.ds(at + GROUP, LANES)]
    values = qkv_ref[rows, pl.ds(at + 2 * GROUP, LANES)]
    query = qkv_ref[win, pl.ds(at, LANES)]
    grad = grad_ref[win, pl.ds(pl.multiple_of(g * GROUP + c, LANES), LANES)]
    dk, dv, dq = [], [], 0.0
    for h in range(2):
        one = pl.ds(4 * g + 2 * pair + h, 1)
        key = keys * scaled[h]
        scores = dot_last(key, query) + bias_ref[:, :cols]
        probs = jnp.exp(scores - lse_ref[one, win])
        dv.append(dot_plain(probs.astype(bf16), grad))
        grad_probs = dot_last(values * plain[h], grad)
        ds = (probs * (grad_probs - inner_ref[one, win])).astype(bf16)
        dk.append(dot_plain(ds, query))
        dq = dq + dot_first(ds, key)
    dq_ref[win, pl.ds(c, LANES)] += dq
    dqkv_ref[rows, pl.ds(GROUP + c, LANES)] = (jnp.where(low, dk[0], dk[1]) * 0.125).astype(bf16)
    dqkv_ref[rows, pl.ds(2 * GROUP + c, LANES)] = jnp.where(low, dv[0], dv[1]).astype(bf16)


def backward_kernel(
    net,
    clip_ref, grad_middle_ref, mixed_ref, qkv_hbm, lse_ref, normed_hbm, tokens_hbm, weights_hbm, gains_ref,
    *refs,
):
    total, width = mixed_ref.shape
    ends = clip_ends(clip_ref)
    refs, load_sem, store_sem = refs[:-2], *refs[-2:]
    refs, (qkv_ref, normed_ref, group_ref, sum_ref) = refs[:-4], refs[-4:]

    def load(slot, start, size):
        return pltpu.make_async_copy(
            weights_hbm.at[:, pl.ds(start, size)], group_ref.at[slot, :, pl.ds(0, size)], load_sem.at[slot]
        )

    weight = load(0, 0, width)
    weight.start()
    inputs = [
        pltpu.make_async_copy(qkv_hbm, qkv_ref, load_sem.at[2]),
        pltpu.make_async_copy(normed_hbm, normed_ref, load_sem.at[3]),
    ]
    for copy in inputs:
        copy.start()
    if net is None:
        grads_ref, grad_tokens_ref, low_ref, grad_ref, dqkv_ref, dq_ref, stat_ref, inner_ref, bias_ref = refs
        plan = {}
    else:
        sums_ref, feed_grads_ref, *owned = refs[:6]
        early, refs = refs[6 : 6 + 2 * EARLY], refs[2 * EARLY :]
        *outs, grad_tokens_ref = refs[6:14]
        low_ref, grad_ref, dqkv_ref, dq_ref, stat_ref, inner_ref, bias_ref, grads_ref, own_ref = refs[14:23]
        shard_ref, shard_feed_ref, send, recv, local, *bufs = refs[23:]
        net.locate()
        net.enter()
        sems = Sems(send, recv)
        feed, att = [], []
        flip = BOTH[::-1]
        for k in range(EARLY):
            for lanes, along in feed_folds(k):
                slots, bufs = [None, early[len(feed)], *bufs[:2]], bufs[2:]
                feed.append(Fold(net, sems, None, flip, lanes, along, slots, shard_feed_ref, steps=(2, 3)))
        span = 2 * GROUP * EARLY
        for k in range(EARLY, feed_grads_ref.shape[-1] // (2 * GROUP)):
            for lanes, along in feed_folds(k):

                def kept(index, start=lanes[0] - span):
                    return own_ref[index + (slice(None), pl.ds(start, GROUP))]

                feed.append(
                    Fold(net, sems, feed_grads_ref, flip, lanes, along, bufs[:4], shard_feed_ref, own=kept)
                )
                bufs = bufs[4:]
        for lanes, along in att_folds(width):
            att.append(Fold(net, sems, grads_ref, BOTH, lanes, along, bufs[:4], shard_ref))
            bufs = bufs[4:]
        early, late = feed[: 2 * EARLY], feed[2 * EARLY :]
        for p in late:
            p.send(0)
        for p in early:
            p.send(2)
        mine = tuple(net.place["c"] if n == "c" else slice(None) for n in net.names(flip))
        own = pltpu.make_async_copy(
            feed_grads_ref.at[mine + (slice(None), pl.ds(span, feed_grads_ref.shape[-1] - span))], own_ref, local
        )
        own.start()
        tall = jnp.concatenate([sums_ref[...], jnp.zeros((LANES - 8, width), f32)], axis=0).T
        lane = lax.broadcasted_iota(jnp.int32, (1, LANES), 1)
        for j in range(1, 4):
            tall = jnp.where(lane == j, jnp.sum(sums_ref[j : j + 1, :], axis=1, keepdims=True), tall)
        extras = jnp.where(lane == 4, ends[-1].astype(f32), tall)

    def advance(*moves):
        for piece, step in moves:
            piece.add(step)
            if step < 3:
                piece.send(step + 1)

    def store(lanes, value):
        if net is None:
            grads_ref[:, lanes] = value.astype(bf16)
        else:
            rows = grads_ref.shape[-2]
            for i, index in enumerate(np.ndindex(*net.dims(BOTH))):
                grads_ref[index + (slice(None), lanes)] = value[i * rows : (i + 1) * rows].astype(bf16)

    if net is not None:
        store(slice(width, width + LANES), extras)
    low_ref[...] = grad_middle_ref[...].astype(bf16)
    store(slice(0, width), dot_first(mixed_ref[...], low_ref[...]))
    weight.wait()
    grad_ref[...] = dot_last(low_ref[...], group_ref[0]).astype(bf16)
    weight = load(1, group_lanes(width, 0).start, 3 * GROUP)
    weight.start()
    tokens_ref = low_ref
    tokens = pltpu.make_async_copy(tokens_hbm, tokens_ref, load_sem.at[4])
    tokens.start()
    inner_sums(grad_ref, mixed_ref, stat_ref)
    inner_ref[...] = stat_ref[...].T[: inner_ref.shape[0]]
    if net is not None:
        for p in att[:2]:
            p.send(0)
        own.wait()
        plan = {
            (0, 0): [(p, 0) for p in late] + [(p, 2) for p in early],
            (0, 1): [(p, 0) for p in att[0:2]],
            (1, 0): [(p, 1) for p in late] + [(p, 1) for p in att[0:2]],
            (1, 1): [(p, 0) for p in att[2:4]],
            (1, 3): [(p, 2) for p in late] + [(p, 2) for p in att[0:2]] + [(p, 1) for p in att[2:4]],
            (2, 0): [(p, 3) for p in early],
            (2, 1): [(p, 0) for p in att[4:6]] + [(p, 2) for p in att[2:4]],
            (2, 3): [(p, 1) for p in att[4:6]] + [(p, 3) for p in late] + [(p, 3) for p in att[0:2]],
        }
    for copy in inputs:
        copy.wait()
    sum_ref[...] = jnp.zeros_like(sum_ref)
    groups = width // GROUP

    def group(g, carry):
        dq_ref[...] = jnp.zeros_like(dq_ref)

        def step(i, carry):
            for (a, b), moves in plan.items():
                pl.when((g == a) & (i == b))(lambda moves=moves: advance(*moves))
            pair_back(
                g, i // 2, i % 2, total, qkv_ref, ends, grad_ref, lse_ref, inner_ref, dqkv_ref, bias_ref, dq_ref
            )
            return carry

        lax.fori_loop(0, 2 * total // WIDE, step, 0)
        dqkv_ref[:, :GROUP] = dq_ref[...].astype(bf16)
        start = width + LANES + g * 3 * GROUP
        store(pl.ds(pl.multiple_of(start, LANES), 3 * GROUP), dot_first(normed_ref[...], dqkv_ref[...]))
        if net is not None:
            for k in range(groups):

                @pl.when(g == k)
                def _(k=k):
                    for p in att[2 + 2 * k : 4 + 2 * k]:
                        p.send(0)

        slot = 1 - lax.rem(g, 2)
        load(slot, 0, 3 * GROUP).wait()
        sum_ref[...] += dot_last(dqkv_ref[...], group_ref[slot])

        @pl.when(g + 1 < groups)
        def _():
            load(1 - slot, pl.multiple_of(start + 3 * GROUP, LANES), 3 * GROUP).start()

        return carry

    lax.fori_loop(0, groups, group, 0)
    if net is not None:
        advance((att[6], 0), (att[7], 0))
    tokens.wait()
    finals = []
    for b in range(total // BLOCK):
        rows = pl.ds(b * BLOCK, BLOCK)
        unit, inv = unit_of(tokens_ref[rows, :].astype(f32))
        sum_ref[rows, :] = grad_middle_ref[rows, :] + unit_back(sum_ref[rows, :], unit, inv, gains_ref[0:1, :])
        finals.append(pltpu.make_async_copy(sum_ref.at[rows], grad_tokens_ref.at[rows], store_sem.at[b]))
        finals[-1].start()
    if net is not None:
        advance((att[6], 1), (att[7], 1), (att[4], 2), (att[5], 2), (att[2], 3), (att[3], 3))
        advance((att[6], 2), (att[7], 2), (att[4], 3), (att[5], 3))
        query_ref, key_ref, value_ref, output_ref, expand_ref, reduce_ref, tile_ref = outs
        output_ref[...] = shard_ref[:, :width]
        for k in range(expand_ref.shape[1] // GROUP):
            cols = slice(k * GROUP, (k + 1) * GROUP)
            expand_ref[:, cols] = shard_feed_ref[:, 2 * k * GROUP : (2 * k + 1) * GROUP]
            reduce_ref[cols, :] = shard_feed_ref[:, (2 * k + 1) * GROUP : (2 * k + 2) * GROUP].T
        advance((att[6], 3), (att[7], 3))
        gain = 0.0
        for j, (out, weight) in enumerate(zip((query_ref, key_ref, value_ref), owned)):
            for g in range(width // GROUP):
                at = width + LANES + (3 * g + j) * GROUP
                out[:, g * GROUP : (g + 1) * GROUP] = shard_ref[:, at : at + GROUP]
            gain = gain + jnp.sum(weight[...].astype(f32) * out[...], axis=1, keepdims=True)
        gain = gain / owned[3][:, :1].astype(f32)
        lane = lax.broadcasted_iota(jnp.int32, (1, LANES), 1)
        tile = shard_ref[:, width : width + LANES]
        means = jnp.sqrt(tile / (tile[:, 4:5] * width))
        tile_ref[...] = jnp.where(lane == LANES - 1, gain, jnp.where(lane == 0, tile, means))
        for p in feed + att:
            p.drain()
    for copy in finals:
        copy.wait()


def params(**more):
    return pltpu.CompilerParams(vmem_limit_bytes=58 << 20, **more)


def shape(*dims, kind=bf16):
    return jax.ShapeDtypeStruct(dims, kind)


def run_forward(clip, tokens, weights, gains):
    total, width = tokens.shape
    return pl.pallas_call(
        forward_kernel,
        name="layer_forward",
        out_shape=(
            shape(total, 3 * width), shape(total, width), shape(16, total, kind=f32),
            shape(total, width, kind=f32), shape(total, width), shape(total, width), shape(8, width, kind=f32),
        ),
        in_specs=[SM, VM, VM, VM],
        out_specs=(VM,) * 7,
        scratch_shapes=[pltpu.VMEM((total, LANES), f32), pltpu.VMEM((BLOCK, total), f32)],
        compiler_params=params(),
        cost_estimate=pl.CostEstimate(flops=12 * 10**9, bytes_accessed=20 << 20, transcendentals=0),
    )(clip, tokens, weights, gains)


def run_feed(clip, feed, out_grad, middle, gains, weights):
    total, width = feed.shape
    parts, _, both = weights.shape
    one = pl.BlockSpec((1, width, both), lambda t: (t, 0, 0))
    return pl.pallas_call(
        feed_kernel,
        name="feed_both",
        grid=(parts,),
        out_shape=(
            shape(parts, width, both), shape(total, width), shape(total, width, kind=f32), shape(8, width, kind=f32),
        ),
        in_specs=[SM, VM, VM, VM, VM, one],
        out_specs=(one, VM, VM, VM),
        scratch_shapes=[
            pltpu.VMEM((total, width), bf16), pltpu.VMEM((total, both - width), bf16),
            pltpu.VMEM((total, both - width), bf16), pltpu.VMEM((total, width), f32), pltpu.VMEM((total, width), f32),
        ],
        compiler_params=params(),
        cost_estimate=pl.CostEstimate(flops=30 * 10**9, bytes_accessed=30 << 20, transcendentals=0),
    )(clip, feed, out_grad, middle, gains, weights)


MESH = pl.DeviceIdType.MESH
ANY = pl.BlockSpec(memory_space=pl.ANY)
FACTORS = {
    (8, 4): ((("z", 4), ("y", 2)), (("x", 2), ("c", 2))),
}


class Net:
    def __init__(self, factors):
        self.factors = factors
        self.size = {n: s for axis in factors for n, s in axis}
        self.count = 1
        for s in self.size.values():
            self.count *= s

    def locate(self):
        self.place = {}
        for name, axis in zip(BOTH, self.factors):
            left = lax.axis_index(name)
            for n, s in axis[::-1]:
                self.place[n] = lax.rem(left, s)
                left = lax.div(left, s)

    def device(self, dim, value):
        out = []
        for axis in self.factors:
            index = 0
            for n, s in axis:
                index = index * s + (value if n == dim else self.place[n])
            out.append(index)
        return tuple(out)

    def names(self, order):
        axes = dict(zip(BOTH, self.factors))
        return [n for a in order for n, _ in axes[a]]

    def dims(self, order):
        return tuple(self.size[n] for n in self.names(order))

    def view(self, ref, order, lanes, **fixed):
        index = tuple(fixed.get(n, slice(None)) for n in self.names(order))
        return ref.at[index + (slice(None), pl.ds(*lanes))]

    def peers(self, dim):
        s = self.size[dim]
        return [lax.rem(self.place[dim] + o, s) for o in range(1, s)]

    def enter(self):
        barrier, count = pltpu.get_barrier_semaphore(), 0
        for dim in self.size:
            for v in self.peers(dim):
                pl.semaphore_signal(barrier, inc=1, device_id=self.device(dim, v), device_id_type=MESH)
                count += 1
        pl.semaphore_wait(barrier, count)


class Sems:
    def __init__(self, send, recv):
        self.send, self.recv, self.used = send, recv, 0

    def take(self):
        self.used += 1
        return self.send.at[self.used - 1], self.recv.at[self.used - 1]


def spread(net, sems, dim, source, target):
    out = []
    for v in net.peers(dim):
        send, recv = sems.take()
        out.append(
            pltpu.make_async_remote_copy(
                src_ref=source, dst_ref=target, send_sem=send, recv_sem=recv,
                device_id=net.device(dim, v), device_id_type=MESH,
            )
        )
    return out


def begin(copies):
    for copy in copies:
        copy.start()


def arrive(copies):
    for copy in copies:
        copy.wait_recv()


class Piece:
    def __init__(self, net, sems, mine, ref, order, lanes, first, second):
        def block(free, **other):
            fixed = {n: v for n, v in net.place.items() if n not in free}
            return net.view(ref, order, lanes, **{**fixed, **other})

        def pass_on(dim, part):
            return spread(net, sems, dim, part, part)

        self.z = spread(net, sems, "z", mine.at[:, pl.ds(*lanes)], block(()))
        self.one = pass_on(first, block(("z",)))
        self.two = pass_on(second, block(("z", first)))
        self.twins = [
            pass_on("c", block(("z",))),
            sum((pass_on("c", block(("z",), **{first: v})) for v in net.peers(first)), []),
            sum((pass_on("c", block(("z", first), **{second: v})) for v in net.peers(second)), []),
        ]

    def start(self):
        begin(self.z)

    def step_one(self):
        arrive(self.z)
        begin(self.one + self.twins[0])

    def step_two(self):
        arrive(self.one)
        begin(self.two + self.twins[1])

    def step_three(self):
        arrive(self.two)
        begin(self.twins[2])

    def ready(self):
        arrive(sum(self.twins, []))

    def drain(self):
        for copy in self.z + self.one + self.two + sum(self.twins, []):
            copy.wait_send()


def copies_of(net):
    z, y, x, c = (net.size[n] - 1 for n in "zyxc")
    return z + y + x + c * (1 + y + x)


def lane_parts(width, count):
    tiles, out, at = width // LANES, [], 0
    for i in range(count):
        take = (tiles - at) // (count - i)
        out.append((at * LANES, take * LANES))
        at += take
    return out


ORDERS = (("y", "x"), ("x", "y"))


def att_spans(width):
    start = width + LANES
    spans = [(width, LANES + 3 * GROUP)]
    spans += [(start + g * 3 * GROUP, 3 * GROUP) for g in range(1, width // GROUP)]
    return spans + [(0, width)]


def halves(start, size):
    return [(start + at, take) for at, take in lane_parts(size, 2)]


def fused_forward_kernel(
    net,
    clip_ref, tokens_ref, w_reduce_ref, out_grad_ref, w_query_ref, w_key_ref, w_value_ref, w_output_ref, gain_ref,
    w_expand_ref,
    att_all, feed_all, qkv_hbm, mixed_hbm, lse_ref, normed_hbm, grads_ref, result_hbm, grad_middle_hbm, sums_ref,
    gains_ref, half_0, half_1, half_2, half_3, qkv_ref, mixed_ref, normed_ref, result_ref, grad_middle_ref, store_sem, mine_ref, both_ref, gain_tile_ref, group_ref, grad_ref, middle_ref, feed_ref, active_ref, hidden_ref, out_ref,
    chunk_ref, stage_ref, stat_ref, bias_ref, send, recv, local, chunk_sem, stage_sem, *early,
):
    total, width = tokens_ref.shape
    groups = width // GROUP
    hid = w_expand_ref.shape[1]
    chunks = hid // GROUP
    ends = clip_ends(clip_ref)
    flip = BOTH[::-1]
    net.locate()

    moves = [(w_output_ref, mine_ref.at[:, pl.ds(0, width)]), (gain_ref, mine_ref.at[:, pl.ds(width, LANES)])]
    for g in range(groups):
        for j, ref in enumerate((w_query_ref, w_key_ref, w_value_ref)):
            at = width + LANES + (3 * g + j) * GROUP
            moves.append((ref.at[:, pl.ds(g * GROUP, GROUP)], mine_ref.at[:, pl.ds(at, GROUP)]))
    for k in range(chunks):
        moves.append((w_expand_ref.at[:, pl.ds(k * GROUP, GROUP)], both_ref.at[:, pl.ds(2 * k * GROUP, GROUP)]))
    copies = [pltpu.make_async_copy(src, dst, local.at[i]) for i, (src, dst) in enumerate(moves)]
    used = len(copies)
    copies.append(pltpu.make_async_copy(out_grad_ref, grad_ref, local.at[used]))
    for copy in copies:
        copy.start()
    turned = w_reduce_ref[...].T
    for k in range(chunks):
        both_ref[:, (2 * k + 1) * GROUP : (2 * k + 2) * GROUP] = turned[:, k * GROUP : (k + 1) * GROUP]
    for copy in copies[:used]:
        copy.wait()
    net.enter()
    sems = Sems(send, recv)
    att = [
        [Piece(net, sems, mine_ref, att_all, BOTH, lanes, *ORDERS[i]) for i, lanes in enumerate(halves(*span))]
        for span in att_spans(width)
    ]
    feed = [
        [
            Piece(net, sems, both_ref, feed_all, flip, lanes, *ORDERS[i])
            for i, lanes in enumerate(halves(2 * k * GROUP, 2 * GROUP))
        ]
        for k in range(chunks)
    ]
    folds = []
    for k in range(EARLY):
        for kind, (lanes, along) in enumerate(feed_folds(k)):

            def staged(index, kind=kind):
                at = dict(zip([n for n in net.names(flip) if n != "c"], index))
                q = at["x"] * net.size["c"] + net.place["c"]
                return stage_ref[kind, at["z"], at["y"], :, pl.ds(pl.multiple_of(q * GROUP, GROUP), GROUP)]

            bufs, early = early[:2], early[2:]
            folds.append(Fold(net, sems, grads_ref, flip, lanes, along, bufs, own=staged, steps=(0, 1)))
    own = [
        pltpu.make_async_copy(mine_ref, net.view(att_all, BOTH, (0, mine_ref.shape[1]), **net.place), local.at[0]),
        pltpu.make_async_copy(both_ref, net.view(feed_all, flip, (0, both_ref.shape[1]), **net.place), local.at[1]),
    ]
    for copy in own:
        copy.start()

    def act(*moves):
        for name, pair in moves:
            for piece in pair:
                getattr(piece, name)()

    first, *others, last = att
    act(("start", first), ("start", others[0]))
    sums_ref[...] = jnp.zeros_like(sums_ref)
    copies[used].wait()
    for copy in own:
        copy.wait()

    def norm(r0):
        rows = pl.ds(r0, BLOCK)
        x = tokens_ref[rows, :].astype(f32)
        valid = valid_of(r0, BLOCK, ends)
        middle_ref[rows, :] = unit_of(x)[0]
        grad_ref[rows, :] = (grad_ref[rows, :].astype(f32) * valid).astype(bf16)
        set_row(sums_ref, 1, jnp.sum(x * x * valid, axis=0, keepdims=True))

    row_loop(total, BLOCK, norm)
    act(("step_one", first), ("start", others[1]), ("start", last))
    act(("step_one", others[0]), ("step_two", first), ("start", feed[0]))
    act(("step_one", others[1]), ("step_two", others[0]), ("step_three", first), ("ready", first))

    def fetch(lanes, target, sem):
        return pltpu.make_async_copy(net.view(att_all, BOTH, lanes), target, sem)

    def flat(value):
        return value.reshape(width, value.shape[-1])

    tile = fetch((width, LANES), gain_tile_ref, local.at[0])
    tile.start()
    weight = fetch((width + LANES, 3 * GROUP), group_ref.at[0], local.at[1])
    weight.start()
    tile.wait()
    gains_ref[...] = flat(gain_tile_ref[...].astype(f32)).T[:8]

    def scale(r0):
        rows = pl.ds(r0, BLOCK)
        normed_ref[rows, :] = (middle_ref[rows, :] * gains_ref[0:1, :]).astype(bf16)

    row_loop(total, BLOCK, scale)
    plan = {
        (0, 0): [("step_one", last), ("step_two", others[1]), ("step_three", others[0])],
        (0, 2): [("step_two", last), ("step_one", feed[0]), ("start", feed[1]), ("ready", others[0])],
        (0, 3): [("step_three", others[1])],
        (1, 0): [("step_three", last), ("step_two", feed[0]), ("ready", others[1])],
        (1, 2): [("step_one", feed[1]), ("start", feed[2]), ("ready", last)],
        (2, 0): [("step_three", feed[0]), ("step_two", feed[1])],
        (2, 2): [("step_one", feed[2])],
    }
    def group(g, carry):
        slot = lax.rem(g, 2)
        fetch((0, 3 * GROUP), group_ref.at[slot], local.at[1]).wait()
        at = pl.multiple_of(g * 3 * GROUP, LANES)
        qkv_ref[:, pl.ds(at, 3 * GROUP)] = dot_plain(normed_ref[...], flat(group_ref[slot])).astype(bf16)

        def step(i, carry):
            for (a, b), todo in plan.items():
                pl.when((g == a) & (i == b))(lambda todo=todo: act(*todo))
            pair_forward(g, i // 2, i % 2, total, qkv_ref, ends, mixed_ref, stat_ref, bias_ref)
            return carry

        lax.fori_loop(0, 2 * total // WIDE, step, 0)
        start = pl.multiple_of(jnp.where(g + 1 < groups, width + LANES + (g + 1) * 3 * GROUP, 0), LANES)
        fetch((start, 3 * GROUP), group_ref.at[1 - slot], local.at[1]).start()
        return carry

    lax.fori_loop(0, groups, group, 0)
    outs = [
        pltpu.make_async_copy(ref, target, store_sem.at[i])
        for i, (ref, target) in enumerate(((qkv_ref, qkv_hbm), (mixed_ref, mixed_hbm), (normed_ref, normed_hbm)))
    ]
    for copy in outs:
        copy.start()
    lse_ref[...] = stat_ref[...].T[: lse_ref.shape[0]]
    fetch((0, 3 * GROUP), group_ref.at[groups % 2], local.at[1]).wait()
    middle_ref[...] = dot_plain(mixed_ref[...], flat(group_ref[groups % 2]))

    def second(r0):
        rows = pl.ds(r0, BLOCK)
        branch = middle_ref[rows, :]
        middle = tokens_ref[rows, :].astype(f32) + branch
        middle_ref[rows, :] = middle
        feed_ref[rows, :] = (unit_of(middle)[0] * gains_ref[1:2, :]).astype(bf16)
        set_row(sums_ref, 2, jnp.sum(branch * branch * valid_of(r0, BLOCK, ends), axis=0, keepdims=True))

    row_loop(total, BLOCK, second)
    act(("ready", feed[0]), ("step_three", feed[1]), ("step_two", feed[2]))

    tp = net.names(("tp",))
    quarters = list(np.ndindex(*(net.size[n] for n in tp)))
    both_kinds = range(2)

    def place(ref, quarter, kind, k):
        at = (2 * k + kind) * GROUP
        at = at if isinstance(at, int) else pl.multiple_of(at, GROUP)
        return ref.at[quarter + (slice(None),) * (len(ref.shape) - len(quarter) - 1) + (pl.ds(at, GROUP),)]

    def part(ref, q):
        return ref.at[(slice(None),) * (len(ref.shape) - 1) + (pl.ds(q * GROUP, GROUP),)]

    def chunk_copies(k, slot):
        return [
            pltpu.make_async_copy(
                place(feed_all, quarter, kind, k), part(chunk_ref.at[slot, kind], q), chunk_sem.at[slot, kind, q]
            )
            for kind in both_kinds
            for q, quarter in enumerate(quarters)
        ]

    def stage_copies(k):
        return [
            pltpu.make_async_copy(part(stage_ref.at[kind], q), place(grads_ref, quarter, kind, k), stage_sem.at[kind, q])
            for kind in both_kinds
            for q, quarter in enumerate(quarters)
        ]

    for copy in chunk_copies(0, 0):
        copy.start()
    out_ref[...] = jnp.zeros_like(out_ref)
    grad_middle_ref[...] = jnp.zeros_like(grad_middle_ref)

    def chunk(k, carry):
        slot = lax.rem(k, 2)
        for copy in chunk_copies(k, slot):
            copy.wait()

        def weights(kind):
            return chunk_ref[slot, kind].reshape(width, len(quarters) * GROUP)

        for q in range(len(quarters)):
            cols = slice(q * GROUP, (q + 1) * GROUP)
            hidden = dot_plain(feed_ref[...], weights(0)[:, cols])
            grad_active = dot_plain(grad_ref[...], weights(1)[:, cols])
            share = 0.5 * (1.0 + lax.erf(hidden * 0.7071067811865476))
            active_ref[:, cols] = (hidden * share).astype(bf16)
            slope = share + hidden * (jnp.exp(-0.5 * hidden * hidden) * 0.3989422804014327)
            hidden_ref[:, cols] = (grad_active * slope).astype(bf16)
        for j in range(chunks - 1):

            @pl.when(k == j)
            def _(j=j):
                if j + 2 < chunks:
                    act(("ready", feed[j + 1]), ("step_three", feed[j + 2]))
                else:
                    act(("ready", feed[j + 1]))
                for copy in chunk_copies(j + 1, (j + 1) % 2):
                    copy.start()

        @pl.when(k > 0)
        def _():
            for copy in stage_copies(k - 1):
                copy.wait()

        for j in range(EARLY):

            @pl.when(k == j + 1)
            def _(j=j):
                for p in folds[2 * j : 2 * j + 2]:
                    p.send(0)

        out_ref[...] += dot_last(active_ref[...], weights(1))
        grad_middle_ref[...] += dot_last(hidden_ref[...], weights(0))
        for j in range(EARLY):

            @pl.when(k == j + 1)
            def _(j=j):
                for p in folds[2 * j : 2 * j + 2]:
                    p.add(0)
                    p.send(1)

        for kind, (left, right) in enumerate(((feed_ref, hidden_ref), (grad_ref, active_ref))):
            stage_ref[kind] = dot_first(left[...], right[...]).reshape(stage_ref.shape[1:]).astype(bf16)
        for copy in stage_copies(k):
            copy.start()
        return carry

    lax.fori_loop(0, chunks, chunk, 0)

    for i in range(total // BLOCK):
        rows = pl.ds(i * BLOCK, BLOCK)
        middle, out, back = middle_ref[rows, :], out_ref[rows, :], grad_middle_ref[rows, :]
        result_ref[rows, :] = (middle + out).astype(bf16)
        unit, inv = unit_of(middle)
        grad_middle_ref[rows, :] = grad_ref[rows, :].astype(f32) + unit_back(back, unit, inv, gains_ref[1:2, :])
        set_row(sums_ref, 3, jnp.sum(out * out * valid_of(i * BLOCK, BLOCK, ends), axis=0, keepdims=True))
        set_row(sums_ref, 0, jnp.sum(back * unit, axis=0, keepdims=True))
        for j, (ref, target) in enumerate(((result_ref, result_hbm), (grad_middle_ref, grad_middle_hbm))):
            outs.append(pltpu.make_async_copy(ref.at[rows], target.at[rows], store_sem.at[3 + 2 * i + j]))
            outs[-1].start()
    for i, (p, target) in enumerate(zip(folds, (half_0, half_1, half_2, half_3))):
        p.add(1)
        outs.append(pltpu.make_async_copy(p.bufs[1].at[pl.ds(0, 1)], target, local.at[i]))
        outs[-1].start()
    for copy in outs:
        copy.wait()
    for copy in stage_copies(chunks - 1):
        copy.wait()
    for p in folds:
        p.drain()
    for pair in att + feed:
        for piece in pair:
            piece.drain()


def run_fused_forward(net, clip, tokens, out_grad, weights, gain_tile, w_expand, w_reduce):
    total, width = tokens.shape
    rows, rows_feed = width // net.count, w_expand.shape[0]
    lanes, hid = 4 * width + LANES, w_expand.shape[1]
    flip = BOTH[::-1]
    ff = (*net.dims(flip), rows_feed, 2 * hid)
    wide = GROUP * int(np.prod(net.dims(("tp",))))
    inner = tuple(net.size[n] for n in net.names(("dp",))) + (rows_feed, wide)
    count = 2 * (len(att_spans(width)) + hid // GROUP) * copies_of(net) + 4 * EARLY * max(net.size.values())
    dma = pltpu.SemaphoreType.DMA
    early, halves_out = [], []
    for k in range(EARLY):
        for fold in feed_folds(k):
            shapes = Fold.shapes(net, flip, rows_feed, *fold)[:2]
            early += [pltpu.VMEM(dims, bf16) for dims in shapes]
            halves_out.append(shape(1, *shapes[1][1:]))
    return pl.pallas_call(
        lambda *refs: fused_forward_kernel(net, *refs),
        name="layer_forward_feed",
        out_shape=(
            shape(*net.dims(BOTH), rows, lanes), shape(*ff), shape(total, 3 * width), shape(total, width),
            shape(16, total, kind=f32), shape(total, width), shape(*ff), shape(total, width),
            shape(total, width, kind=f32), shape(8, width, kind=f32), shape(8, width, kind=f32), *halves_out,
        ),
        in_specs=[SM, VM, VM] + [ANY] * 7,
        out_specs=(ANY, ANY, ANY, ANY, VM, ANY, ANY, ANY, ANY, VM, VM) + (ANY,) * len(halves_out),
        scratch_shapes=[
            pltpu.VMEM((total, 3 * width), bf16), pltpu.VMEM((total, width), bf16), pltpu.VMEM((total, width), bf16),
            pltpu.VMEM((total, width), bf16), pltpu.VMEM((total, width), f32), dma((3 + 2 * total // BLOCK,)),
            pltpu.VMEM((rows, lanes), bf16), pltpu.VMEM((rows_feed, 2 * hid), bf16), pltpu.VMEM((*net.dims(BOTH), rows, LANES), bf16),
            pltpu.VMEM((2, *net.dims(BOTH), rows, 3 * GROUP), bf16), pltpu.VMEM((total, width), bf16),
            pltpu.VMEM((total, width), f32), pltpu.VMEM((total, width), bf16), pltpu.VMEM((total, wide), bf16),
            pltpu.VMEM((total, wide), bf16), pltpu.VMEM((total, width), f32), pltpu.VMEM((2, 2, *inner), bf16),
            pltpu.VMEM((2, *inner), bf16), pltpu.VMEM((total, LANES), f32),
            pltpu.VMEM((WIDE, static_windows(total)[1]), f32),
            dma((count,)), dma((count,)),
            dma((4 + 3 * (width // GROUP) + hid // GROUP,)), dma((2, 2, wide // GROUP)), dma((2, wide // GROUP)),
            *early,
        ],
        compiler_params=params(collective_id=1, has_side_effects=True),
    )(clip, tokens, w_reduce, out_grad, *weights, gain_tile, w_expand)


def store_at(ref, index, lanes, value):
    ref[tuple(index) + (slice(None), lanes)] = value


def each(dims, body, index=()):
    count = 1
    for size in dims:
        count *= size
    if count <= 4:
        for tail in np.ndindex(*dims):
            body(index + tail)
    else:

        def step(i, carry):
            each(dims[1:], body, index + (i,))
            return carry

        lax.fori_loop(0, dims[0], step, 0)


class Fold:
    def __init__(self, net, sems, ref, order, lanes, along, bufs, out=None, own=None, steps=(0, 1, 2, 3)):
        self.net, self.lanes, self.along, self.bufs, self.out, self.steps = net, lanes, along, bufs, out, steps
        names = net.names(order)
        self.names = [[n for n in names if n not in along[:k]] for k in range(5)]
        self.ref, self.own = ref, own
        self.copies = {}
        for k in steps:
            dim = along[k]
            source, cols = (ref, lanes) if k == 0 else (bufs[k - 1].at[0], (0, lanes[1]))
            self.copies[k] = []
            for o, v in enumerate(net.peers(dim)):
                index = tuple(v if n == dim else slice(None) for n in self.names[k])
                s, r = sems.take()
                self.copies[k].append(
                    pltpu.make_async_remote_copy(
                        src_ref=source.at[index + (slice(None), pl.ds(*cols))], dst_ref=bufs[k].at[o],
                        send_sem=s, recv_sem=r, device_id=net.device(dim, v), device_id_type=MESH,
                    )
                )

    @staticmethod
    def shapes(net, order, rows, lanes, along):
        names, out = net.names(order), []
        for k, dim in enumerate(along):
            left = [net.size[n] for n in names if n not in along[: k + 1]]
            out.append((net.size[dim] - 1, *left, rows, lanes[1]))
        return out

    def send(self, k):
        begin(self.copies[k])

    def add(self, k):
        arrive(self.copies[k])
        dim, buf, cols = self.along[k], self.bufs[k], slice(0, self.lanes[1])
        here = self.net.place[dim]
        wide = pl.ds(*self.lanes)

        def one(index):
            at = dict(zip(self.names[k + 1], index))
            full = tuple(at.get(n, here) for n in self.names[k])
            if k > 0:
                total = self.bufs[k - 1][(0,) + full + (slice(None), cols)].astype(f32)
            elif self.own is not None:
                total = self.own(index).astype(f32)
            else:
                total = self.ref[full + (slice(None), wide)].astype(f32)
            terms = [total] + [buf[(o,) + index].astype(f32) for o in range(self.net.size[dim] - 1)]
            if len(terms) > 2:
                size = len(terms)
                total = 0.0
                for v in range(size):
                    back = lax.rem(here - v + size, size)
                    term = terms[0]
                    for o in range(1, size):
                        term = jnp.where(back == o, terms[o], term)
                    total = total + term
            else:
                total = terms[0] + terms[1]
            if k == 3:
                self.out[:, wide] = total
            else:
                buf[(0,) + index] = total.astype(bf16)

        each([self.net.size[n] for n in self.names[k + 1]], one)

    def drain(self):
        for copies in self.copies.values():
            for copy in copies:
                copy.wait_send()


ALONG = (("c", "x", "y", "z"), ("c", "y", "x", "z"))


def feed_folds(k):
    return [((2 * GROUP * k + GROUP * i, GROUP), ALONG[i]) for i in range(2)]


EARLY = 2


def att_folds(width):
    out = []
    spans = [(0, width + LANES)] + [(width + LANES + g * 3 * GROUP, 3 * GROUP) for g in range(width // GROUP)]
    for start, size in spans:
        for i, (at, take) in enumerate(lane_parts(size, 2)):
            out.append(((start + at, take), ALONG[i % 2]))
    return out


def run_backward(net, clip, grad_middle, mixed, qkv, lse, normed, tokens, weights, gains, *more_args):
    total, width = tokens.shape
    lanes = weights.shape[1]
    scratch = [
        pltpu.VMEM((total, width), bf16), pltpu.VMEM((total, width), bf16), pltpu.VMEM((total, 3 * GROUP), bf16),
        pltpu.VMEM((total, GROUP), f32), pltpu.VMEM((total, LANES), f32), pltpu.VMEM((16, total), f32),
        pltpu.VMEM((WIDE, static_windows(total)[1]), f32),
    ]
    operands = [clip, grad_middle, mixed, qkv, lse, normed, tokens, weights, gains]
    in_specs = [SM, VM, VM, ANY, VM, ANY, ANY, ANY, VM]
    out_shape = (shape(width, lanes), shape(total, width, kind=f32))
    more = {}
    if net is not None:
        feed_grads = more_args[1]
        rows, rows_feed = width // net.count, feed_grads.shape[-2]
        hid = feed_grads.shape[-1] // 2
        flip = BOTH[::-1]
        operands += more_args
        in_specs += [VM, ANY] + [VM] * (4 + 2 * EARLY)
        out_shape = (
            *(shape(rows, width, kind=f32) for _ in range(4)), shape(rows_feed, hid, kind=f32),
            shape(hid, rows_feed, kind=f32), shape(rows, LANES, kind=f32), out_shape[1],
        )
        scratch.append(pltpu.VMEM((*net.dims(BOTH), rows, lanes), bf16))
        kept = tuple(net.size[n] for n in net.names(flip) if n != "c")
        scratch.append(pltpu.VMEM((*kept, rows_feed, 2 * hid - 2 * GROUP * EARLY), bf16))
        scratch += [pltpu.VMEM((rows, lanes), f32), pltpu.VMEM((rows_feed, 2 * hid), f32)]
        bufs = []
        for k in range(hid // GROUP):
            for f in feed_folds(k):
                bufs += Fold.shapes(net, flip, rows_feed, *f)[2 if k < EARLY else 0 :]
        for f in att_folds(width):
            bufs += Fold.shapes(net, BOTH, rows, *f)
        count = sum(dims[0] for dims in bufs)
        scratch += [pltpu.SemaphoreType.DMA((count,)), pltpu.SemaphoreType.DMA((count,)), pltpu.SemaphoreType.DMA]
        scratch += [pltpu.VMEM(dims, bf16) for dims in bufs]
        more = dict(collective_id=2, has_side_effects=True)
    scratch += [
        pltpu.VMEM((total, 3 * width), bf16), pltpu.VMEM((total, width), bf16),
        pltpu.VMEM((2, width, 3 * GROUP), bf16), pltpu.VMEM((total, width), f32),
        pltpu.SemaphoreType.DMA((5,)), pltpu.SemaphoreType.DMA((total // BLOCK,)),
    ]
    return pl.pallas_call(
        lambda *refs: backward_kernel(net, *refs),
        name="layer_backward",
        out_shape=out_shape,
        in_specs=in_specs,
        out_specs=(VM,) * (len(out_shape) - 1) + (ANY,),
        scratch_shapes=scratch,
        compiler_params=params(**more),
        cost_estimate=pl.CostEstimate(flops=22 * 10**9, bytes_accessed=30 << 20, transcendentals=0),
    )(*operands)


def on_device(
    net,
    tokens, clip_lengths, out_grad, w_query, w_key, w_value, w_output, gain_attention, gain_feed, w_expand, w_reduce,
):
    _, total, width = tokens.shape
    rows = tokens.reshape(total, width)
    out_grad = out_grad.reshape(total, width)
    gain_tile = jnp.pad(jnp.stack([gain_attention, gain_feed], axis=1), ((0, 0), (0, LANES - 2)))
    hid = w_expand.shape[1]
    if net is not None:
        weights, _, qkv, mixed, lse, normed, feed_grads, result, grad_middle, sums, gains, *early = run_fused_forward(
            net, clip_lengths, rows, out_grad, (w_query, w_key, w_value, w_output), gain_tile, w_expand, w_reduce
        )
        weights = weights.reshape(width, -1)
        query, key, value, output, expand, reduce, tile, grad_tokens = run_backward(
            net, clip_lengths, grad_middle, mixed, qkv, lse, normed, rows, weights, gains, sums, feed_grads,
            w_query, w_key, w_value, gain_tile, *early,
        )
        gain_one, gain_two, means = tile[:, LANES - 1], tile[:, 0], tile[0, 1:4]
    else:
        mine = [w_output, gain_tile]
        for g in range(width // GROUP):
            mine += [w[:, g * GROUP : (g + 1) * GROUP] for w in (w_query, w_key, w_value)]
        weights = lax.all_gather(jnp.concatenate(mine, axis=1), BOTH, axis=0, tiled=True)
        both = jnp.concatenate([w_expand, w_reduce.T], axis=1)
        feed_weights = lax.all_gather(both, BOTH[::-1], axis=0, tiled=True).reshape(-1, width, 2 * hid)
        gains = jnp.pad(weights[:, width : width + 2].T.astype(f32), ((0, 6), (0, 0)))
        qkv, mixed, lse, middle, feed, normed, sums_one = run_forward(clip_lengths, rows, weights, gains)
        feed_grads, result, grad_middle, sums_two = run_feed(
            clip_lengths, feed, out_grad, middle, gains, feed_weights
        )
        count = jnp.sum(clip_lengths[:, : SLOTS - 1]).astype(f32)
        squares = jnp.stack([jnp.sum(sums_one[0]), jnp.sum(sums_one[1]), jnp.sum(sums_two[0]), count])
        grads, grad_tokens = run_backward(
            None, clip_lengths, grad_middle, mixed, qkv, lse, normed, rows, weights, gains
        )
        shard = lax.psum_scatter(grads, BOTH, scatter_dimension=0, tiled=True).astype(f32)
        shard_feed = lax.psum_scatter(
            feed_grads.reshape(-1, 2 * hid), BOTH[::-1], scatter_dimension=0, tiled=True
        ).astype(f32)
        stats = lax.psum(squares, BOTH)
        gain_two = lax.psum_scatter(sums_two[1], BOTH, scatter_dimension=0, tiled=True)
        means = jnp.sqrt(stats[:3] / (stats[3] * width))
        parts = shard[:, width + LANES :].reshape(-1, width // GROUP, 3, GROUP)
        query, key, value = (parts[:, :, j].reshape(-1, width) for j in range(3))
        pairs = ((w_query, query), (w_key, key), (w_value, value))
        gain_one = sum(jnp.sum(w.astype(f32) * g, axis=1) for w, g in pairs) / gain_attention.astype(f32)
        output, expand, reduce = shard[:, :width], shard_feed[:, :hid], shard_feed[:, hid:].T
    return (
        result.reshape(1, total, width),
        grad_tokens.reshape(1, total, width),
        query,
        key,
        value,
        output,
        gain_one,
        gain_two,
        expand,
        reduce,
        means,
    )


def solution(mesh):
    row, flat = P(BOTH, None), P(BOTH)
    whole = P(BOTH, None, None)
    in_specs = (whole, row, whole, row, row, row, row, flat, flat, P("dp", "tp"), P("tp", "dp"))
    out_specs = (whole, whole, row, row, row, row, flat, flat, P("dp", "tp"), P("tp", "dp"), P())
    factors = FACTORS.get((mesh.shape["dp"], mesh.shape["tp"]))
    net = Net(factors) if factors else None
    return jax.shard_map(
        lambda *args: on_device(net, *args), mesh=mesh, in_specs=in_specs, out_specs=out_specs, check_vma=False
    )
```

profile of v0, /device:TPU:0, one launch (start us, length us, event | category | flops | bytes accessed | tf_op | source)
XLA Modules:
  0.0 222.4 jit_solution(7949428399588988566)
XLA Ops:
  0.6 0.7 pad_maximum_fusion
  1.3 0.1 copy.30
  1.4 0.6 pad.4.refs_8_.refs_14_
  2.0 1.7 copy.31.refs_2_
  3.8 125.4 %layer_forward_feed.1 = (bf16[4,2,2,2,24,3200]{5,4,3,2,1,0:T(8,128)(2,1)}, bf16[2,2,4,2,96,1536]{5,4,3,2,1,0:T(8,128)(2,1)}, bf16[1024,2304]{1,0:T(8,128)(2,1)},...) custom-call(s32[1,4]{1,0:T(1,128)} %refs_0_.3, ...), custom_call_target="tpu_custom_call" | custom-call | tf_op jit(solution)/shard_map/layer_forward_feed/pallas_call | solution.py:1025
  129.2 80.8 %layer_backward.1 = (f32[24,768]{1,0:T(8,128)}, f32[24,768]{1,0:T(8,128)}, f32[24,768]{1,0:T(8,128)}, f32[24,768]{1,0:T(8,128)}, f32[96,768]{1,0:T(8,128)}, /*in...) custom-call(s32[1,4]{1,0:T(1,128)} %refs_0_.3, f32[1024,768]{1,0:T(8,128)} %get-tuple-element.34.refs_1_, ...), custom_call_target="tpu_custom_call" | custom-call | flops 22000001024 | bytes 31457280 | tf_op jit(solution)/shard_map/layer_backward/pallas_call | solution.py:1205
  210.0 0.0 copy-start
  210.0 1.4 slice_bitcast_fusion
  211.4 1.5 slice_reduce_fusion
  212.9 1.9 copy.32
  214.8 2.7 %copy.40 = bf16[1,1024,768]{2,1,0:T(8,128)(2,1)} copy(bf16[1,1024,768]{2,1,0:T(8,128)(2,1)} %bitcast.13) | data formatting | bytes 3145728
  217.4 0.0 copy-done
  217.4 0.0 copy-start.5
  217.4 0.0 copy-start.4
  217.4 0.0 copy-start.3
  217.4 0.0 copy-start.2
  217.5 0.0 copy-start.1
  217.5 1.7 copy.41
  219.1 0.0 copy-done.5
  219.1 0.6 copy.42
  219.8 0.0 copy-done.4
  219.8 0.6 copy.43
  220.4 0.0 copy-done.3
  220.4 0.6 copy.44
  221.0 0.0 copy-done.2
  221.0 0.6 copy.45
  221.7 0.0 copy-done.1
  221.7 0.7 copy.46
Async XLA Ops:
  210.0 7.4 %copy-start = (f32[1024,768]{1,0:T(8,128)S(1)}, f32[1024,768]{1,0:T(8,128)}, u32[]{:S(2)}) copy-start(f32[1024,768]{1,0:T(8,128)} %get-tuple-element.47) | copy-start | bytes 9437188
  217.4 1.7 copy-start.5
  217.4 2.3 %copy-start.4 = (f32[24,768]{1,0:T(8,128)S(1)}, f32[24,768]{1,0:T(8,128)}, u32[]{:S(2)}) copy-start(f32[24,768]{1,0:T(8,128)} %get-tuple-element.104) | copy-start | bytes 221188
  217.4 3.0 %copy-start.3 = (f32[24,768]{1,0:T(8,128)S(1)}, f32[24,768]{1,0:T(8,128)}, u32[]{:S(2)}) copy-start(f32[24,768]{1,0:T(8,128)} %get-tuple-element.105) | copy-start | bytes 221188
  217.4 3.6 %copy-start.2 = (f32[24,768]{1,0:T(8,128)S(1)}, f32[24,768]{1,0:T(8,128)}, u32[]{:S(2)}) copy-start(f32[24,768]{1,0:T(8,128)} %get-tuple-element.106) | copy-start | bytes 221188
  217.5 4.2 %copy-start.1 = (f32[96,768]{1,0:T(8,128)S(1)}, f32[96,768]{1,0:T(8,128)}, u32[]{:S(2)}) copy-start(f32[96,768]{1,0:T(8,128)} %get-tuple-element.109) | copy-start | bytes 884740
where the time goes:
time: 223 us; the launch traced here: 222 us
  Pallas kernels  206 us (92%)
  local copies, waits for them, and re-layouts  14.8 us (7%)
    pallas_call x1, Pallas kernels, run_fused_forward(): pl.pallas_call(lambda *refs: fused_forward_kernel(net, *refs), name='laye...  125 us
    pallas_call x1, Pallas kernels, run_backward(): pl.pallas_call(lambda *refs: backward_kernel(net, *refs), name='layer_bac...  80.8 us
    unnamed x21, local copies, waits for them, and re-layouts  11.2 us

commit v1 on v0

--- a/solution.py
+++ b/solution.py
@@ -14,7 +14,10 @@
 WIDE = 512
 MAXCLIP = 384
 GROUP = 256
+TRIO = 3 * LANES
 NEG = -1e30
+LOG2E = 1.4426950408889634
+LN2 = 0.6931471805599453
 f32 = jnp.float32
 bf16 = jnp.bfloat16
 BOTH = ("dp", "tp")
@@ -67,29 +70,6 @@
     return (position < ends[-1]).astype(f32)
 
 
-def window_of(low, high, ends, total):
-    start, stop = jnp.int32(0), jnp.int32(total)
-    for e in ends:
-        start = jnp.where(low >= e, e, start)
-    for e in ends[::-1]:
-        stop = jnp.where(high < e, e, stop)
-    block = start // LANES
-    return block, (stop + LANES - 1) // LANES - block
-
-
-def by_width(block, count, total, run):
-    most = total // LANES
-    widths = [w for w in range(2, most + 1) if w != most - 1]
-    before = 0
-    for w in widths:
-
-        @pl.when((count > before) & (count <= w))
-        def _(w=w):
-            run(pl.multiple_of(jnp.minimum(block, most - w) * LANES, LANES), w * LANES)
-
-        before = w
-
-
 def row_loop(total, size, body):
     def step(i, carry):
         body(pl.multiple_of(i * size, size))
@@ -104,70 +84,57 @@
     return lane, low, (jnp.where(low, scale, 0.0).astype(bf16), jnp.where(low, 0.0, scale).astype(bf16))
 
 
-def set_bias(bias_ref, row_start, rows, col_start, cols, ends):
-    row_seg = segment_of(row_start + lax.broadcasted_iota(jnp.int32, (rows, 1), 0), ends)
-    col_seg = segment_of(col_start + lax.broadcasted_iota(jnp.int32, (1, cols), 1), ends)
-    bias_ref[:, :cols] = jnp.where(row_seg == col_seg, 0.0, NEG)
-
-
-def attend(qkv_ref, ends, mixed_ref, stat_ref, bias_ref):
-    total, width = mixed_ref.shape
-    lane, low, scaled = head_masks(0.125)
+def lane_index():
+    lane = lax.broadcasted_iota(jnp.int32, (1, LANES), 1)
+    return lane, lax.rem(lane, HEAD_DIM)
+
+
+def split_three(value):
+    high = value.astype(bf16)
+    rest = value - high.astype(f32)
+    middle = rest.astype(bf16)
+    return high, middle, (rest - middle.astype(f32)).astype(bf16)
+
+
+def in_lanes(at, first, terms, other):
+    out = other
+    for i, term in enumerate(terms):
+        out = jnp.where(at == first + i, term.astype(f32), out)
+    return out
+
+
+def set_codes(query_ref, key_ref, ends):
+    _, at = lane_index()
 
     def block(r0):
         rows = pl.ds(r0, BLOCK)
-
-        def run(k0, cols):
-            win = pl.ds(k0, cols)
-            set_bias(bias_ref, r0, BLOCK, k0, cols, ends)
-
-            def pair(p, carry):
-                c = pl.multiple_of(p * LANES, LANES)
-                at = pl.multiple_of(p // 2 * (3 * GROUP) + p % 2 * LANES, LANES)
-                query = qkv_ref[rows, pl.ds(at, LANES)]
-                keys = qkv_ref[win, pl.ds(at + GROUP, LANES)]
-                values = qkv_ref[win, pl.ds(at + 2 * GROUP, LANES)]
-                values = jnp.concatenate([values, jnp.ones_like(values)], axis=1)
-                stats, outs = stat_ref[rows, :], []
-                for h, mask in enumerate(scaled):
-                    scores = dot_last(query * mask, keys) + bias_ref[:, :cols]
-                    top = jnp.max(scores, axis=1, keepdims=True)
-                    mixed = dot_plain(jnp.exp(scores - top).astype(bf16), values)
-                    row_sum = mixed[:, LANES:]
-                    outs.append(mixed[:, :LANES] / row_sum)
-                    stats = jnp.where(lane == 2 * p + h, top + jnp.log(row_sum), stats)
-                stat_ref[rows, :] = stats
-                mixed_ref[rows, pl.ds(c, LANES)] = jnp.where(low, outs[0], outs[1]).astype(bf16)
-                return carry
-
-            lax.fori_loop(0, width // LANES, pair, 0)
-
-        by_width(*window_of(r0, r0 + BLOCK - 1, ends, total), total, run)
-
-    row_loop(total, BLOCK, block)
-
-
-def inner_sums(grad_ref, mixed_ref, stat_ref):
+        seg = segment_of(r0 + lax.broadcasted_iota(jnp.int32, (BLOCK, 1), 0), ends)
+        own = at == seg
+        if query_ref is not None:
+            query_ref[rows, :] = jnp.where(own, NEG, 0.0).astype(bf16)
+        key_ref[rows, :] = jnp.where((at < SLOTS + 3) & jnp.logical_not(own), 1.0, 0.0).astype(bf16)
+
+    row_loop(key_ref.shape[0], BLOCK, block)
+
+
+def inner_codes(grad_ref, mixed_ref, out_ref):
     total, width = mixed_ref.shape
-    lane, low, _ = head_masks(1.0)
+    _, at = lane_index()
+    _, low, _ = head_masks(1.0)
 
     def block(r0):
         rows = pl.ds(r0, LANES)
-        sums = jnp.zeros((LANES, LANES), f32)
         for p in range(width // LANES):
             cols = slice(p * LANES, (p + 1) * LANES)
             both = grad_ref[rows, cols].astype(f32) * mixed_ref[rows, cols].astype(f32)
-            first = jnp.sum(jnp.where(low, both, 0.0), axis=1, keepdims=True)
-            second = jnp.sum(jnp.where(low, 0.0, both), axis=1, keepdims=True)
-            sums = jnp.where(lane == 2 * p, first, jnp.where(lane == 2 * p + 1, second, sums))
-        stat_ref[rows, :] = sums
+            sums = (
+                jnp.sum(jnp.where(low, both, 0.0), axis=1, keepdims=True),
+                jnp.sum(jnp.where(low, 0.0, both), axis=1, keepdims=True),
+            )
+            first, second = (in_lanes(at, 0, split_three(-x), 0.0) for x in sums)
+            out_ref[rows, cols] = jnp.where(low, second, first).astype(bf16)
 
     row_loop(total, LANES, block)
-
-
-def group_lanes(width, g):
-    start = width + LANES + g * 3 * GROUP
-    return slice(start, start + 3 * GROUP)
 
 
 def set_row(ref, row, value):
@@ -177,8 +144,8 @@
 
 def forward_kernel(
     clip_ref, tokens_ref, weights_ref, gains_ref,
-    qkv_ref, mixed_ref, lse_ref, middle_ref, feed_ref, normed_ref, sums_ref,
-    stat_ref, bias_ref,
+    qkv_ref, mixed_ref, extra_ref, middle_ref, feed_ref, normed_ref, sums_ref,
+    code_q_ref, code_k_ref,
 ):
     total, width = tokens_ref.shape
     ends = clip_ends(clip_ref)
@@ -191,11 +158,19 @@
         set_row(sums_ref, 0, jnp.sum(x * x * valid_of(r0, BLOCK, ends), axis=0, keepdims=True))
 
     row_loop(total, BLOCK, norm)
-    for g in range(width // GROUP):
-        cols = slice(g * 3 * GROUP, (g + 1) * 3 * GROUP)
-        qkv_ref[:, cols] = dot_plain(normed_ref[...], weights_ref[:, group_lanes(width, g)]).astype(bf16)
-    attend(qkv_ref, ends, mixed_ref, stat_ref, bias_ref)
-    lse_ref[...] = stat_ref[...].T[: lse_ref.shape[0]]
+    set_codes(code_q_ref, code_k_ref, ends)
+    for p in range(width // LANES):
+        weight = weights_ref[:, width + LANES + p * TRIO : width + LANES + (p + 1) * TRIO]
+        project(normed_ref, pl.ds(0, total), weight, qkv_ref, p)
+
+    def pair_block(i, carry):
+        blocks = total // WIDE
+        pair_forward(
+            lax.div(i, blocks), lax.rem(i, blocks), total, qkv_ref, mixed_ref, extra_ref, code_q_ref, code_k_ref
+        )
+        return carry
+
+    lax.fori_loop(0, width // LANES * (total // WIDE), pair_block, 0)
     middle_ref[...] = dot_plain(mixed_ref[...], weights_ref[:, :width])
 
     def second(r0):
@@ -280,103 +255,101 @@
     return pl.multiple_of(at, LANES)
 
 
-def pair_forward(g, block, pair, total, qkv_ref, ends, mixed_ref, stat_ref, bias_ref):
+def pair_parts(p, block, total):
     starts, cols = static_windows(total)
-    lane, low, scaled = head_masks(0.125)
-    r0 = pl.multiple_of(block * WIDE, WIDE)
-    k0 = start_of(starts, block)
-    rows, win = pl.ds(r0, WIDE), pl.ds(k0, cols)
-
-    @pl.when(pair == 0)
-    def _():
-        set_bias(bias_ref, r0, WIDE, k0, cols, ends)
-
-    c = pl.multiple_of(pair * LANES, LANES)
-    at = pl.multiple_of(g * 3 * GROUP + c, LANES)
-    query = qkv_ref[rows, pl.ds(at, LANES)]
-    keys = qkv_ref[win, pl.ds(at + GROUP, LANES)]
-    values = qkv_ref[win, pl.ds(at + 2 * GROUP, LANES)]
+    rows = pl.ds(pl.multiple_of(block * WIDE, WIDE), WIDE)
+    win = pl.ds(start_of(starts, block), cols)
+    return rows, win, [pl.ds(pl.multiple_of(p * TRIO + j * LANES, LANES), LANES) for j in range(3)]
+
+
+def with_codes(value, code, plain):
+    return value * plain[0] + code * plain[1], value * plain[1] + code * plain[0]
+
+
+def pair_forward(p, block, total, qkv_ref, mixed_ref, extra_ref, code_q_ref, code_k_ref):
+    _, at = lane_index()
+    _, low, plain = head_masks(1.0)
+    rows, win, (at_q, at_k, at_v) = pair_parts(p, block, total)
+    query, keys, values = qkv_ref[rows, at_q], qkv_ref[win, at_k], qkv_ref[win, at_v]
     values = jnp.concatenate([values, jnp.ones_like(values)], axis=1)
-    stats, outs = stat_ref[rows, :], []
-    for h, mask in enumerate(scaled):
-        scores = dot_last(query * mask, keys) + bias_ref[:, :cols]
+    code = code_q_ref[rows, :]
+    queries, keys = with_codes(query, code, plain), with_codes(keys, code_k_ref[win, :], plain)
+    outs, extras = [], []
+    for h in range(2):
+        scores = dot_last(queries[h], keys[h])
         top = jnp.max(scores, axis=1, keepdims=True)
-        mixed = dot_plain(jnp.exp(scores - top).astype(bf16), values)
+        mixed = dot_plain(jnp.exp2(scores - top).astype(bf16), values)
         row_sum = mixed[:, LANES:]
         outs.append(mixed[:, :LANES] / row_sum)
-        stats = jnp.where(lane == 4 * g + 2 * pair + h, top + jnp.log(row_sum), stats)
-    stat_ref[rows, :] = stats
-    mixed_ref[rows, pl.ds(pl.multiple_of(g * GROUP + c, LANES), LANES)] = jnp.where(low, outs[0], outs[1]).astype(bf16)
-
-
-def pair_back(g, block, pair, total, qkv_ref, ends, grad_ref, lse_ref, inner_ref, dqkv_ref, bias_ref, dq_ref):
-    starts, cols = static_windows(total)
+        extras.append(in_lanes(at, SLOTS, split_three(-(top + LOG2E * jnp.log(row_sum))), code.astype(f32)))
+    lanes = pl.ds(pl.multiple_of(p * LANES, LANES), LANES)
+    mixed_ref[rows, lanes] = jnp.where(low, outs[0], outs[1]).astype(bf16)
+    extra_ref[rows, lanes] = jnp.where(low, extras[1], extras[0]).astype(bf16)
+
+
+def pair_back(p, block, total, qkv_ref, grad_ref, extra_ref, inner_ref, code_k_ref, dqkv_ref, dq_ref):
+    _, at = lane_index()
     _, low, scaled = head_masks(0.125)
     _, _, plain = head_masks(1.0)
-    r0 = pl.multiple_of(block * WIDE, WIDE)
-    q0 = start_of(starts, block)
-    rows, win = pl.ds(r0, WIDE), pl.ds(q0, cols)
-
-    @pl.when(pair == 0)
-    def _():
-        set_bias(bias_ref, r0, WIDE, q0, cols, ends)
-
-    c = pl.multiple_of(pair * LANES, LANES)
-    at = pl.multiple_of(g * 3 * GROUP + c, LANES)
-    keys = qkv_ref[rows, pl.ds(at + GROUP, LANES)]
-    values = qkv_ref[rows, pl.ds(at + 2 * GROUP, LANES)]
-    query = qkv_ref[win, pl.ds(at, LANES)]
-    grad = grad_ref[win, pl.ds(pl.multiple_of(g * GROUP + c, LANES), LANES)]
+    rows, win, (at_q, at_k, at_v) = pair_parts(p, block, total)
+    lanes = pl.ds(pl.multiple_of(p * LANES, LANES), LANES)
+    keys, values, query, grad = qkv_ref[rows, at_k], qkv_ref[rows, at_v], qkv_ref[win, at_q], grad_ref[win, lanes]
+    ones = jnp.where(at < 3, 1.0, 0.0).astype(bf16)
+    key_codes, query_codes = with_codes(keys, code_k_ref[rows, :], plain), with_codes(query, extra_ref[win, lanes], plain)
+    value_codes, grad_codes = with_codes(values, ones, plain), with_codes(grad, inner_ref[win, lanes], plain)
     dk, dv, dq = [], [], 0.0
     for h in range(2):
-        one = pl.ds(4 * g + 2 * pair + h, 1)
-        key = keys * scaled[h]
-        scores = dot_last(key, query) + bias_ref[:, :cols]
-        probs = jnp.exp(scores - lse_ref[one, win])
+        probs = jnp.exp2(dot_last(key_codes[h], query_codes[h]))
         dv.append(dot_plain(probs.astype(bf16), grad))
-        grad_probs = dot_last(values * plain[h], grad)
-        ds = (probs * (grad_probs - inner_ref[one, win])).astype(bf16)
+        ds = (probs * dot_last(value_codes[h], grad_codes[h])).astype(bf16)
         dk.append(dot_plain(ds, query))
-        dq = dq + dot_first(ds, key)
-    dq_ref[win, pl.ds(c, LANES)] += dq
-    dqkv_ref[rows, pl.ds(GROUP + c, LANES)] = (jnp.where(low, dk[0], dk[1]) * 0.125).astype(bf16)
-    dqkv_ref[rows, pl.ds(2 * GROUP + c, LANES)] = jnp.where(low, dv[0], dv[1]).astype(bf16)
+        dq = dq + dot_first(ds, keys * scaled[h])
+    dq_ref[win, :] += dq
+    dqkv_ref[rows, at_k] = (jnp.where(low, dk[0], dk[1]) * LN2).astype(bf16)
+    dqkv_ref[rows, at_v] = jnp.where(low, dv[0], dv[1]).astype(bf16)
+
+
+def project(normed_ref, rows, weight, qkv_ref, p):
+    lane = lax.broadcasted_iota(jnp.int32, (1, TRIO), 1)
+    scale = jnp.where(lane < LANES, 0.125 * LOG2E, 1.0)
+    at = pl.multiple_of(p * TRIO, LANES)
+    qkv_ref[rows, pl.ds(at, TRIO)] = (dot_plain(normed_ref[rows, :], weight) * scale).astype(bf16)
 
 
 def backward_kernel(
     net,
-    clip_ref, grad_middle_ref, mixed_ref, qkv_hbm, lse_ref, normed_hbm, tokens_hbm, weights_hbm, gains_ref,
+    clip_ref, grad_middle_ref, mixed_ref, qkv_hbm, extra_hbm, normed_hbm, tokens_hbm, weights_hbm, gains_ref,
     *refs,
 ):
     total, width = mixed_ref.shape
     ends = clip_ends(clip_ref)
     refs, load_sem, store_sem = refs[:-2], *refs[-2:]
-    refs, (qkv_ref, normed_ref, group_ref, sum_ref) = refs[:-4], refs[-4:]
-
-    def load(slot, start, size):
-        return pltpu.make_async_copy(
-            weights_hbm.at[:, pl.ds(start, size)], group_ref.at[slot, :, pl.ds(0, size)], load_sem.at[slot]
+    refs, (qkv_ref, extra_ref, normed_ref, output_weight_ref, weight_ref, sum_ref) = refs[:-6], refs[-6:]
+    pairs = width // LANES
+    loads = [
+        pltpu.make_async_copy(source, target, load_sem.at[i])
+        for i, (source, target) in enumerate(
+            (
+                (weights_hbm.at[:, pl.ds(0, width)], output_weight_ref),
+                (qkv_hbm, qkv_ref),
+                (extra_hbm, extra_ref),
+                (normed_hbm, normed_ref),
+                (weights_hbm.at[:, pl.ds(width + LANES, pairs * TRIO)], weight_ref),
+            )
         )
-
-    weight = load(0, 0, width)
-    weight.start()
-    inputs = [
-        pltpu.make_async_copy(qkv_hbm, qkv_ref, load_sem.at[2]),
-        pltpu.make_async_copy(normed_hbm, normed_ref, load_sem.at[3]),
     ]
-    for copy in inputs:
-        copy.start()
+    begin(loads)
     if net is None:
-        grads_ref, grad_tokens_ref, low_ref, grad_ref, dqkv_ref, dq_ref, stat_ref, inner_ref, bias_ref = refs
+        grads_ref, grad_tokens_ref, low_ref, grad_ref, dqkv_ref, dq_ref, inner_ref, code_k_ref = refs
         plan = {}
     else:
-        sums_ref, feed_grads_ref, *owned = refs[:6]
-        early, refs = refs[6 : 6 + 2 * EARLY], refs[2 * EARLY :]
-        *outs, grad_tokens_ref = refs[6:14]
-        low_ref, grad_ref, dqkv_ref, dq_ref, stat_ref, inner_ref, bias_ref, grads_ref, own_ref = refs[14:23]
-        shard_ref, shard_feed_ref, send, recv, local, *bufs = refs[23:]
+        sums_ref, feed_grads_ref, *refs = refs
+        early, refs = refs[: 2 * EARLY], refs[2 * EARLY :]
+        shard_ref, shard_feed_ref, grad_tokens_ref, low_ref, grad_ref, dqkv_ref, dq_ref, inner_ref, *refs = refs
+        code_k_ref, grads_ref, own_ref, send, recv, local, *bufs = refs
         net.locate()
-        net.enter()
+        net.announce()
+        net.meet()
         sems = Sems(send, recv)
         feed, att = [], []
         flip = BOTH[::-1]
@@ -414,11 +387,12 @@
             tall = jnp.where(lane == j, jnp.sum(sums_ref[j : j + 1, :], axis=1, keepdims=True), tall)
         extras = jnp.where(lane == 4, ends[-1].astype(f32), tall)
 
-    def advance(*moves):
-        for piece, step in moves:
-            piece.add(step)
-            if step < 3:
-                piece.send(step + 1)
+    def advance(*todo):
+        for pieces, step in todo:
+            for piece in pieces:
+                piece.add(step)
+                if step < 3:
+                    piece.send(step + 1)
 
     def store(lanes, value):
         if net is None:
@@ -432,70 +406,79 @@
         store(slice(width, width + LANES), extras)
     low_ref[...] = grad_middle_ref[...].astype(bf16)
     store(slice(0, width), dot_first(mixed_ref[...], low_ref[...]))
-    weight.wait()
-    grad_ref[...] = dot_last(low_ref[...], group_ref[0]).astype(bf16)
-    weight = load(1, group_lanes(width, 0).start, 3 * GROUP)
-    weight.start()
-    tokens_ref = low_ref
-    tokens = pltpu.make_async_copy(tokens_hbm, tokens_ref, load_sem.at[4])
-    tokens.start()
-    inner_sums(grad_ref, mixed_ref, stat_ref)
-    inner_ref[...] = stat_ref[...].T[: inner_ref.shape[0]]
     if net is not None:
         for p in att[:2]:
             p.send(0)
+    loads[0].wait()
+    grad_ref[...] = dot_last(low_ref[...], output_weight_ref[...]).astype(bf16)
+    tokens_ref = low_ref
+    tokens = pltpu.make_async_copy(tokens_hbm, tokens_ref, load_sem.at[5])
+    tokens.start()
+    set_codes(None, code_k_ref, ends)
+    inner_codes(grad_ref, mixed_ref, inner_ref)
+    moves, ending = {}, {}
+    if net is not None:
         own.wait()
-        plan = {
-            (0, 0): [(p, 0) for p in late] + [(p, 2) for p in early],
-            (0, 1): [(p, 0) for p in att[0:2]],
-            (1, 0): [(p, 1) for p in late] + [(p, 1) for p in att[0:2]],
-            (1, 1): [(p, 0) for p in att[2:4]],
-            (1, 3): [(p, 2) for p in late] + [(p, 2) for p in att[0:2]] + [(p, 1) for p in att[2:4]],
-            (2, 0): [(p, 3) for p in early],
-            (2, 1): [(p, 0) for p in att[4:6]] + [(p, 2) for p in att[2:4]],
-            (2, 3): [(p, 1) for p in att[4:6]] + [(p, 3) for p in late] + [(p, 3) for p in att[0:2]],
+        output, pair = att[:2], [att[2 + 2 * p : 4 + 2 * p] for p in range(pairs)]
+        moves = {
+            0: [(late, 0)],
+            1: [(output, 0)],
+            2: [(early, 2)],
+            3: [(pair[0], 0)],
+            4: [(late, 1), (output, 1)],
+            5: [(pair[1], 0), (pair[0], 1)],
+            6: [(output, 2)],
+            7: [(pair[2], 0), (pair[1], 1), (late, 2), (pair[0], 2)],
+            8: [(early, 3)],
+            9: [(pair[3], 0), (pair[2], 1), (pair[1], 2)],
+            10: [(output, 3), (pair[0], 3)],
+            11: [(pair[4], 0), (pair[3], 1), (pair[2], 2), (late, 3)],
         }
-    for copy in inputs:
+        ending = {
+            0: [(pair[4], 1), (pair[3], 2), (pair[1], 3)],
+            1: [(pair[5], 0)],
+            2: [(pair[2], 3)],
+            4: [(pair[4], 2)],
+            6: [(pair[5], 1), (pair[3], 3)],
+        }
+    for copy in loads[1:]:
         copy.wait()
-    sum_ref[...] = jnp.zeros_like(sum_ref)
-    groups = width // GROUP
-
-    def group(g, carry):
+    blocks = total // WIDE
+
+    def per_pair(p, carry):
         dq_ref[...] = jnp.zeros_like(dq_ref)
 
-        def step(i, carry):
-            for (a, b), moves in plan.items():
-                pl.when((g == a) & (i == b))(lambda moves=moves: advance(*moves))
-            pair_back(
-                g, i // 2, i % 2, total, qkv_ref, ends, grad_ref, lse_ref, inner_ref, dqkv_ref, bias_ref, dq_ref
-            )
+        def step(b, carry):
+            for i, todo in moves.items():
+                pl.when(p * blocks + b == i)(lambda todo=todo: advance(*todo))
+            pair_back(p, b, total, qkv_ref, grad_ref, extra_ref, inner_ref, code_k_ref, dqkv_ref, dq_ref)
             return carry
 
-        lax.fori_loop(0, 2 * total // WIDE, step, 0)
-        dqkv_ref[:, :GROUP] = dq_ref[...].astype(bf16)
-        start = width + LANES + g * 3 * GROUP
-        store(pl.ds(pl.multiple_of(start, LANES), 3 * GROUP), dot_first(normed_ref[...], dqkv_ref[...]))
+        lax.fori_loop(0, blocks, step, 0)
+        at = pl.multiple_of(p * TRIO, LANES)
+        dqkv_ref[:, pl.ds(at, LANES)] = dq_ref[...].astype(bf16)
+        lanes = pl.ds(pl.multiple_of(width + LANES + at, LANES), TRIO)
+        store(lanes, dot_first(normed_ref[...], dqkv_ref[:, pl.ds(at, TRIO)]))
         if net is not None:
-            for k in range(groups):
-
-                @pl.when(g == k)
+            for k in range(pairs):
+
+                @pl.when(p == k)
                 def _(k=k):
-                    for p in att[2 + 2 * k : 4 + 2 * k]:
-                        p.send(0)
-
-        slot = 1 - lax.rem(g, 2)
-        load(slot, 0, 3 * GROUP).wait()
-        sum_ref[...] += dot_last(dqkv_ref[...], group_ref[slot])
-
-        @pl.when(g + 1 < groups)
-        def _():
-            load(1 - slot, pl.multiple_of(start + 3 * GROUP, LANES), 3 * GROUP).start()
+                    for piece in pair[k]:
+                        piece.send(0)
 
         return carry
 
-    lax.fori_loop(0, groups, group, 0)
-    if net is not None:
-        advance((att[6], 0), (att[7], 0))
+    lax.fori_loop(0, pairs, per_pair, 0)
+    third = pairs * TRIO // 3
+    for j in range(3):
+        cols = slice(j * third, (j + 1) * third)
+        back = dot_last(dqkv_ref[:, cols], weight_ref[:, cols])
+        if j == 0:
+            sum_ref[...] = back
+        else:
+            sum_ref[...] += back
+        advance(*ending.get(j, ()))
     tokens.wait()
     finals = []
     for b in range(total // BLOCK):
@@ -504,27 +487,10 @@
         sum_ref[rows, :] = grad_middle_ref[rows, :] + unit_back(sum_ref[rows, :], unit, inv, gains_ref[0:1, :])
         finals.append(pltpu.make_async_copy(sum_ref.at[rows], grad_tokens_ref.at[rows], store_sem.at[b]))
         finals[-1].start()
+        advance(*ending.get(3 + b, ()))
     if net is not None:
-        advance((att[6], 1), (att[7], 1), (att[4], 2), (att[5], 2), (att[2], 3), (att[3], 3))
-        advance((att[6], 2), (att[7], 2), (att[4], 3), (att[5], 3))
-        query_ref, key_ref, value_ref, output_ref, expand_ref, reduce_ref, tile_ref = outs
-        output_ref[...] = shard_ref[:, :width]
-        for k in range(expand_ref.shape[1] // GROUP):
-            cols = slice(k * GROUP, (k + 1) * GROUP)
-            expand_ref[:, cols] = shard_feed_ref[:, 2 * k * GROUP : (2 * k + 1) * GROUP]
-            reduce_ref[cols, :] = shard_feed_ref[:, (2 * k + 1) * GROUP : (2 * k + 2) * GROUP].T
-        advance((att[6], 3), (att[7], 3))
-        gain = 0.0
-        for j, (out, weight) in enumerate(zip((query_ref, key_ref, value_ref), owned)):
-            for g in range(width // GROUP):
-                at = width + LANES + (3 * g + j) * GROUP
-                out[:, g * GROUP : (g + 1) * GROUP] = shard_ref[:, at : at + GROUP]
-            gain = gain + jnp.sum(weight[...].astype(f32) * out[...], axis=1, keepdims=True)
-        gain = gain / owned[3][:, :1].astype(f32)
-        lane = lax.broadcasted_iota(jnp.int32, (1, LANES), 1)
-        tile = shard_ref[:, width : width + LANES]
-        means = jnp.sqrt(tile / (tile[:, 4:5] * width))
-        tile_ref[...] = jnp.where(lane == LANES - 1, gain, jnp.where(lane == 0, tile, means))
+        advance((pair[5], 2), (pair[4], 3))
+        advance((pair[5], 3))
         for p in feed + att:
             p.drain()
     for copy in finals:
@@ -545,12 +511,12 @@
         forward_kernel,
         name="layer_forward",
         out_shape=(
-            shape(total, 3 * width), shape(total, width), shape(16, total, kind=f32),
+            shape(total, 3 * width), shape(total, width), shape(total, width),
             shape(total, width, kind=f32), shape(total, width), shape(total, width), shape(8, width, kind=f32),
         ),
         in_specs=[SM, VM, VM, VM],
         out_specs=(VM,) * 7,
-        scratch_shapes=[pltpu.VMEM((total, LANES), f32), pltpu.VMEM((BLOCK, total), f32)],
+        scratch_shapes=[pltpu.VMEM((total, LANES), bf16), pltpu.VMEM((total, LANES), bf16)],
         compiler_params=params(),
         cost_estimate=pl.CostEstimate(flops=12 * 10**9, bytes_accessed=20 << 20, transcendentals=0),
     )(clip, tokens, weights, gains)
@@ -625,13 +591,14 @@
         s = self.size[dim]
         return [lax.rem(self.place[dim] + o, s) for o in range(1, s)]
 
-    def enter(self):
-        barrier, count = pltpu.get_barrier_semaphore(), 0
+    def announce(self):
+        barrier = pltpu.get_barrier_semaphore()
         for dim in self.size:
             for v in self.peers(dim):
                 pl.semaphore_signal(barrier, inc=1, device_id=self.device(dim, v), device_id_type=MESH)
-                count += 1
-        pl.semaphore_wait(barrier, count)
+
+    def meet(self):
+        pl.semaphore_wait(pltpu.get_barrier_semaphore(), sum(s - 1 for s in self.size.values()))
 
 
 class Sems:
@@ -675,6 +642,7 @@
         def pass_on(dim, part):
             return spread(net, sems, dim, part, part)
 
+        self.left = False
         self.z = spread(net, sems, "z", mine.at[:, pl.ds(*lanes)], block(()))
         self.one = pass_on(first, block(("z",)))
         self.two = pass_on(second, block(("z", first)))
@@ -687,6 +655,11 @@
     def start(self):
         begin(self.z)
 
+    def leave(self):
+        for copy in self.z:
+            copy.wait_send()
+        self.left = True
+
     def step_one(self):
         arrive(self.z)
         begin(self.one + self.twins[0])
@@ -703,7 +676,7 @@
         arrive(sum(self.twins, []))
 
     def drain(self):
-        for copy in self.z + self.one + self.two + sum(self.twins, []):
+        for copy in ([] if self.left else self.z) + self.one + self.two + sum(self.twins, []):
             copy.wait_send()
 
 
@@ -726,8 +699,7 @@
 
 def att_spans(width):
     start = width + LANES
-    spans = [(width, LANES + 3 * GROUP)]
-    spans += [(start + g * 3 * GROUP, 3 * GROUP) for g in range(1, width // GROUP)]
+    spans = [(width, LANES + TRIO)] + [(start + p * TRIO, TRIO) for p in range(1, width // LANES)]
     return spans + [(0, width)]
 
 
@@ -739,36 +711,35 @@
     net,
     clip_ref, tokens_ref, w_reduce_ref, out_grad_ref, w_query_ref, w_key_ref, w_value_ref, w_output_ref, gain_ref,
     w_expand_ref,
-    att_all, feed_all, qkv_hbm, mixed_hbm, lse_ref, normed_hbm, grads_ref, result_hbm, grad_middle_hbm, sums_ref,
-    gains_ref, half_0, half_1, half_2, half_3, qkv_ref, mixed_ref, normed_ref, result_ref, grad_middle_ref, store_sem, mine_ref, both_ref, gain_tile_ref, group_ref, grad_ref, middle_ref, feed_ref, active_ref, hidden_ref, out_ref,
-    chunk_ref, stage_ref, stat_ref, bias_ref, send, recv, local, chunk_sem, stage_sem, *early,
+    att_all, feed_all, qkv_hbm, mixed_hbm, extra_hbm, normed_hbm, grads_ref, result_hbm, grad_middle_hbm, sums_ref,
+    gains_ref, half_0, half_1, half_2, half_3, qkv_ref, mixed_ref, extra_ref, normed_ref, result_ref, grad_middle_ref, store_sem, mine_ref, both_ref, gain_tile_ref, group_ref, output_weight_ref, grad_ref, middle_ref, feed_ref, active_ref, hidden_ref, out_ref,
+    chunk_ref, stage_ref, code_q_ref, code_k_ref, send, recv, local, chunk_sem, stage_sem, *early,
 ):
     total, width = tokens_ref.shape
-    groups = width // GROUP
+    pairs = width // LANES
     hid = w_expand_ref.shape[1]
     chunks = hid // GROUP
     ends = clip_ends(clip_ref)
     flip = BOTH[::-1]
     net.locate()
+    net.announce()
 
     moves = [(w_output_ref, mine_ref.at[:, pl.ds(0, width)]), (gain_ref, mine_ref.at[:, pl.ds(width, LANES)])]
-    for g in range(groups):
+    for p in range(pairs):
         for j, ref in enumerate((w_query_ref, w_key_ref, w_value_ref)):
-            at = width + LANES + (3 * g + j) * GROUP
-            moves.append((ref.at[:, pl.ds(g * GROUP, GROUP)], mine_ref.at[:, pl.ds(at, GROUP)]))
+            at = width + LANES + p * TRIO + j * LANES
+            moves.append((ref.at[:, pl.ds(p * LANES, LANES)], mine_ref.at[:, pl.ds(at, LANES)]))
     for k in range(chunks):
-        moves.append((w_expand_ref.at[:, pl.ds(k * GROUP, GROUP)], both_ref.at[:, pl.ds(2 * k * GROUP, GROUP)]))
+        for kind, ref in enumerate((w_expand_ref, w_reduce_ref)):
+            moves.append((ref.at[:, pl.ds(k * GROUP, GROUP)], both_ref.at[:, pl.ds((2 * k + kind) * GROUP, GROUP)]))
     copies = [pltpu.make_async_copy(src, dst, local.at[i]) for i, (src, dst) in enumerate(moves)]
     used = len(copies)
     copies.append(pltpu.make_async_copy(out_grad_ref, grad_ref, local.at[used]))
     for copy in copies:
         copy.start()
-    turned = w_reduce_ref[...].T
-    for k in range(chunks):
-        both_ref[:, (2 * k + 1) * GROUP : (2 * k + 2) * GROUP] = turned[:, k * GROUP : (k + 1) * GROUP]
     for copy in copies[:used]:
         copy.wait()
-    net.enter()
+    net.meet()
     sems = Sems(send, recv)
     att = [
         [Piece(net, sems, mine_ref, att_all, BOTH, lanes, *ORDERS[i]) for i, lanes in enumerate(halves(*span))]
@@ -804,8 +775,8 @@
             for piece in pair:
                 getattr(piece, name)()
 
-    first, *others, last = att
-    act(("start", first), ("start", others[0]))
+    pair, output = att[:-1], att[-1]
+    act(("start", pair[0]))
     sums_ref[...] = jnp.zeros_like(sums_ref)
     copies[used].wait()
     for copy in own:
@@ -820,9 +791,14 @@
         set_row(sums_ref, 1, jnp.sum(x * x * valid, axis=0, keepdims=True))
 
     row_loop(total, BLOCK, norm)
-    act(("step_one", first), ("start", others[1]), ("start", last))
-    act(("step_one", others[0]), ("step_two", first), ("start", feed[0]))
-    act(("step_one", others[1]), ("step_two", others[0]), ("step_three", first), ("ready", first))
+    set_codes(code_q_ref, code_k_ref, ends)
+    for p in range(pairs):
+        act(("leave", pair[p]), ("start", pair[p + 1] if p + 1 < pairs else feed[0]), ("step_one", pair[p]))
+        if p >= 2:
+            act(("step_two", pair[p - 2]))
+        if p >= 4:
+            act(("step_three", pair[p - 4]))
+    act(("ready", pair[0]))
 
     def fetch(lanes, target, sem):
         return pltpu.make_async_copy(net.view(att_all, BOTH, lanes), target, sem)
@@ -832,8 +808,7 @@
 
     tile = fetch((width, LANES), gain_tile_ref, local.at[0])
     tile.start()
-    weight = fetch((width + LANES, 3 * GROUP), group_ref.at[0], local.at[1])
-    weight.start()
+    fetch((width + LANES, TRIO), group_ref.at[0], local.at[1]).start()
     tile.wait()
     gains_ref[...] = flat(gain_tile_ref[...].astype(f32)).T[:8]
 
@@ -843,41 +818,52 @@
 
     row_loop(total, BLOCK, scale)
     plan = {
-        (0, 0): [("step_one", last), ("step_two", others[1]), ("step_three", others[0])],
-        (0, 2): [("step_two", last), ("step_one", feed[0]), ("start", feed[1]), ("ready", others[0])],
-        (0, 3): [("step_three", others[1])],
-        (1, 0): [("step_three", last), ("step_two", feed[0]), ("ready", others[1])],
-        (1, 2): [("step_one", feed[1]), ("start", feed[2]), ("ready", last)],
-        (2, 0): [("step_three", feed[0]), ("step_two", feed[1])],
-        (2, 2): [("step_one", feed[2])],
+        0: [("step_two", pair[4]), ("step_three", pair[2]), ("ready", pair[1])],
+        1: [("step_two", pair[5]), ("step_three", pair[3]), ("start", output)],
+        2: [("start", feed[1]), ("step_three", pair[4]), ("ready", pair[2])],
+        3: [("step_one", feed[0]), ("step_three", pair[5])],
+        4: [("step_one", output), ("ready", pair[3])],
+        6: [("step_two", output), ("step_two", feed[0]), ("start", feed[2]), ("ready", pair[4])],
+        8: [("step_one", feed[1]), ("ready", pair[5])],
+        9: [("step_three", output)],
+        11: [("step_three", feed[0])],
     }
-    def group(g, carry):
-        slot = lax.rem(g, 2)
-        fetch((0, 3 * GROUP), group_ref.at[slot], local.at[1]).wait()
-        at = pl.multiple_of(g * 3 * GROUP, LANES)
-        qkv_ref[:, pl.ds(at, 3 * GROUP)] = dot_plain(normed_ref[...], flat(group_ref[slot])).astype(bf16)
-
-        def step(i, carry):
-            for (a, b), todo in plan.items():
-                pl.when((g == a) & (i == b))(lambda todo=todo: act(*todo))
-            pair_forward(g, i // 2, i % 2, total, qkv_ref, ends, mixed_ref, stat_ref, bias_ref)
+    blocks = total // WIDE
+
+    def per_pair(p, carry):
+        slot = lax.rem(p, 2)
+        fetch((0, TRIO), group_ref.at[slot], local.at[1]).wait()
+        project(normed_ref, pl.ds(0, total), flat(group_ref[slot]), qkv_ref, p)
+
+        def step(b, carry):
+            for i, todo in plan.items():
+                pl.when(p * blocks + b == i)(lambda todo=todo: act(*todo))
+
+            @pl.when((b == 1) & (p + 1 < pairs))
+            def _():
+                start = pl.multiple_of(width + LANES + (p + 1) * TRIO, LANES)
+                fetch((start, TRIO), group_ref.at[1 - slot], local.at[1]).start()
+
+            pair_forward(p, b, total, qkv_ref, mixed_ref, extra_ref, code_q_ref, code_k_ref)
             return carry
 
-        lax.fori_loop(0, 2 * total // WIDE, step, 0)
-        start = pl.multiple_of(jnp.where(g + 1 < groups, width + LANES + (g + 1) * 3 * GROUP, 0), LANES)
-        fetch((start, 3 * GROUP), group_ref.at[1 - slot], local.at[1]).start()
+        lax.fori_loop(0, blocks, step, 0)
         return carry
 
-    lax.fori_loop(0, groups, group, 0)
+    lax.fori_loop(0, pairs, per_pair, 0)
+    act(("ready", output))
+    fetch((0, width), output_weight_ref, local.at[1]).start()
     outs = [
         pltpu.make_async_copy(ref, target, store_sem.at[i])
-        for i, (ref, target) in enumerate(((qkv_ref, qkv_hbm), (mixed_ref, mixed_hbm), (normed_ref, normed_hbm)))
+        for i, (ref, target) in enumerate(
+            ((qkv_ref, qkv_hbm), (mixed_ref, mixed_hbm), (normed_ref, normed_hbm), (extra_ref, extra_hbm))
+        )
     ]
     for copy in outs:
         copy.start()
-    lse_ref[...] = stat_ref[...].T[: lse_ref.shape[0]]
-    fetch((0, 3 * GROUP), group_ref.at[groups % 2], local.at[1]).wait()
-    middle_ref[...] = dot_plain(mixed_ref[...], flat(group_ref[groups % 2]))
+    fetch((0, width), output_weight_ref, local.at[1]).wait()
+    middle_ref[...] = dot_plain(mixed_ref[...], flat(output_weight_ref[...]))
+    act(("step_two", feed[1]), ("step_one", feed[2]))
 
     def second(r0):
         rows = pl.ds(r0, BLOCK)
@@ -888,7 +874,8 @@
         set_row(sums_ref, 2, jnp.sum(branch * branch * valid_of(r0, BLOCK, ends), axis=0, keepdims=True))
 
     row_loop(total, BLOCK, second)
-    act(("ready", feed[0]), ("step_three", feed[1]), ("step_two", feed[2]))
+    act(("ready", feed[0]))
+    feed_plan = {(0, 3): [("step_three", feed[1]), ("step_two", feed[2])], (1, 3): [("step_three", feed[2])]}
 
     tp = net.names(("tp",))
     quarters = list(np.ndindex(*(net.size[n] for n in tp)))
@@ -932,6 +919,23 @@
             return chunk_ref[slot, kind].reshape(width, len(quarters) * GROUP)
 
         for q in range(len(quarters)):
+            for (a, b), todo in feed_plan.items():
+                if q == b:
+                    pl.when(k == a)(lambda todo=todo: act(*todo))
+            if q == 1:
+
+                @pl.when(k > 0)
+                def _():
+                    for copy in stage_copies(k - 1):
+                        copy.wait()
+
+                for j in range(EARLY):
+
+                    @pl.when(k == j + 1)
+                    def _(j=j):
+                        for p in folds[2 * j : 2 * j + 2]:
+                            p.send(0)
+
             cols = slice(q * GROUP, (q + 1) * GROUP)
             hidden = dot_plain(feed_ref[...], weights(0)[:, cols])
             grad_active = dot_plain(grad_ref[...], weights(1)[:, cols])
@@ -943,27 +947,10 @@
 
             @pl.when(k == j)
             def _(j=j):
-                if j + 2 < chunks:
-                    act(("ready", feed[j + 1]), ("step_three", feed[j + 2]))
-                else:
-                    act(("ready", feed[j + 1]))
+                act(("ready", feed[j + 1]))
                 for copy in chunk_copies(j + 1, (j + 1) % 2):
                     copy.start()
 
-        @pl.when(k > 0)
-        def _():
-            for copy in stage_copies(k - 1):
-                copy.wait()
-
-        for j in range(EARLY):
-
-            @pl.when(k == j + 1)
-            def _(j=j):
-                for p in folds[2 * j : 2 * j + 2]:
-                    p.send(0)
-
-        out_ref[...] += dot_last(active_ref[...], weights(1))
-        grad_middle_ref[...] += dot_last(hidden_ref[...], weights(0))
         for j in range(EARLY):
 
             @pl.when(k == j + 1)
@@ -972,6 +959,8 @@
                     p.add(0)
                     p.send(1)
 
+        out_ref[...] += dot_last(active_ref[...], weights(1))
+        grad_middle_ref[...] += dot_last(hidden_ref[...], weights(0))
         for kind, (left, right) in enumerate(((feed_ref, hidden_ref), (grad_ref, active_ref))):
             stage_ref[kind] = dot_first(left[...], right[...]).reshape(stage_ref.shape[1:]).astype(bf16)
         for copy in stage_copies(k):
@@ -989,7 +978,7 @@
         set_row(sums_ref, 3, jnp.sum(out * out * valid_of(i * BLOCK, BLOCK, ends), axis=0, keepdims=True))
         set_row(sums_ref, 0, jnp.sum(back * unit, axis=0, keepdims=True))
         for j, (ref, target) in enumerate(((result_ref, result_hbm), (grad_middle_ref, grad_middle_hbm))):
-            outs.append(pltpu.make_async_copy(ref.at[rows], target.at[rows], store_sem.at[3 + 2 * i + j]))
+            outs.append(pltpu.make_async_copy(ref.at[rows], target.at[rows], store_sem.at[4 + 2 * i + j]))
             outs[-1].start()
     for i, (p, target) in enumerate(zip(folds, (half_0, half_1, half_2, half_3))):
         p.add(1)
@@ -1027,22 +1016,22 @@
         name="layer_forward_feed",
         out_shape=(
             shape(*net.dims(BOTH), rows, lanes), shape(*ff), shape(total, 3 * width), shape(total, width),
-            shape(16, total, kind=f32), shape(total, width), shape(*ff), shape(total, width),
+            shape(total, width), shape(total, width), shape(*ff), shape(total, width),
             shape(total, width, kind=f32), shape(8, width, kind=f32), shape(8, width, kind=f32), *halves_out,
         ),
-        in_specs=[SM, VM, VM] + [ANY] * 7,
-        out_specs=(ANY, ANY, ANY, ANY, VM, ANY, ANY, ANY, ANY, VM, VM) + (ANY,) * len(halves_out),
+        in_specs=[SM, VM] + [ANY] * 8,
+        out_specs=(ANY, ANY, ANY, ANY, ANY, ANY, ANY, ANY, ANY, VM, VM) + (ANY,) * len(halves_out),
         scratch_shapes=[
             pltpu.VMEM((total, 3 * width), bf16), pltpu.VMEM((total, width), bf16), pltpu.VMEM((total, width), bf16),
-            pltpu.VMEM((total, width), bf16), pltpu.VMEM((total, width), f32), dma((3 + 2 * total // BLOCK,)),
+            pltpu.VMEM((total, width), bf16), pltpu.VMEM((total, width), bf16), pltpu.VMEM((total, width), f32), dma((4 + 2 * total // BLOCK,)),
             pltpu.VMEM((rows, lanes), bf16), pltpu.VMEM((rows_feed, 2 * hid), bf16), pltpu.VMEM((*net.dims(BOTH), rows, LANES), bf16),
-            pltpu.VMEM((2, *net.dims(BOTH), rows, 3 * GROUP), bf16), pltpu.VMEM((total, width), bf16),
+            pltpu.VMEM((2, *net.dims(BOTH), rows, TRIO), bf16), pltpu.VMEM((*net.dims(BOTH), rows, width), bf16),
+            pltpu.VMEM((total, width), bf16),
             pltpu.VMEM((total, width), f32), pltpu.VMEM((total, width), bf16), pltpu.VMEM((total, wide), bf16),
             pltpu.VMEM((total, wide), bf16), pltpu.VMEM((total, width), f32), pltpu.VMEM((2, 2, *inner), bf16),
-            pltpu.VMEM((2, *inner), bf16), pltpu.VMEM((total, LANES), f32),
-            pltpu.VMEM((WIDE, static_windows(total)[1]), f32),
+            pltpu.VMEM((2, *inner), bf16), pltpu.VMEM((total, LANES), bf16), pltpu.VMEM((total, LANES), bf16),
             dma((count,)), dma((count,)),
-            dma((4 + 3 * (width // GROUP) + hid // GROUP,)), dma((2, 2, wide // GROUP)), dma((2, wide // GROUP)),
+            dma((4 + 3 * (width // LANES) + 2 * hid // GROUP,)), dma((2, 2, wide // GROUP)), dma((2, wide // GROUP)),
             *early,
         ],
         compiler_params=params(collective_id=1, has_side_effects=True),
@@ -1153,23 +1142,22 @@
 
 def att_folds(width):
     out = []
-    spans = [(0, width + LANES)] + [(width + LANES + g * 3 * GROUP, 3 * GROUP) for g in range(width // GROUP)]
+    spans = [(0, width + LANES)] + [(width + LANES + p * TRIO, TRIO) for p in range(width // LANES)]
     for start, size in spans:
         for i, (at, take) in enumerate(lane_parts(size, 2)):
             out.append(((start + at, take), ALONG[i % 2]))
     return out
 
 
-def run_backward(net, clip, grad_middle, mixed, qkv, lse, normed, tokens, weights, gains, *more_args):
+def run_backward(net, clip, grad_middle, mixed, qkv, extra, normed, tokens, weights, gains, *more_args):
     total, width = tokens.shape
     lanes = weights.shape[1]
     scratch = [
-        pltpu.VMEM((total, width), bf16), pltpu.VMEM((total, width), bf16), pltpu.VMEM((total, 3 * GROUP), bf16),
-        pltpu.VMEM((total, GROUP), f32), pltpu.VMEM((total, LANES), f32), pltpu.VMEM((16, total), f32),
-        pltpu.VMEM((WIDE, static_windows(total)[1]), f32),
+        pltpu.VMEM((total, width), bf16), pltpu.VMEM((total, width), bf16), pltpu.VMEM((total, 3 * width), bf16),
+        pltpu.VMEM((total, LANES), f32), pltpu.VMEM((total, width), bf16), pltpu.VMEM((total, LANES), bf16),
     ]
-    operands = [clip, grad_middle, mixed, qkv, lse, normed, tokens, weights, gains]
-    in_specs = [SM, VM, VM, ANY, VM, ANY, ANY, ANY, VM]
+    operands = [clip, grad_middle, mixed, qkv, extra, normed, tokens, weights, gains]
+    in_specs = [SM, VM, VM, ANY, ANY, ANY, ANY, ANY, VM]
     out_shape = (shape(width, lanes), shape(total, width, kind=f32))
     more = {}
     if net is not None:
@@ -1178,15 +1166,11 @@
         hid = feed_grads.shape[-1] // 2
         flip = BOTH[::-1]
         operands += more_args
-        in_specs += [VM, ANY] + [VM] * (4 + 2 * EARLY)
-        out_shape = (
-            *(shape(rows, width, kind=f32) for _ in range(4)), shape(rows_feed, hid, kind=f32),
-            shape(hid, rows_feed, kind=f32), shape(rows, LANES, kind=f32), out_shape[1],
-        )
+        in_specs += [VM, ANY] + [VM] * (2 * EARLY)
+        out_shape = (shape(rows, lanes, kind=f32), shape(rows_feed, 2 * hid, kind=f32), out_shape[1])
         scratch.append(pltpu.VMEM((*net.dims(BOTH), rows, lanes), bf16))
         kept = tuple(net.size[n] for n in net.names(flip) if n != "c")
         scratch.append(pltpu.VMEM((*kept, rows_feed, 2 * hid - 2 * GROUP * EARLY), bf16))
-        scratch += [pltpu.VMEM((rows, lanes), f32), pltpu.VMEM((rows_feed, 2 * hid), f32)]
         bufs = []
         for k in range(hid // GROUP):
             for f in feed_folds(k):
@@ -1198,9 +1182,9 @@
         scratch += [pltpu.VMEM(dims, bf16) for dims in bufs]
         more = dict(collective_id=2, has_side_effects=True)
     scratch += [
-        pltpu.VMEM((total, 3 * width), bf16), pltpu.VMEM((total, width), bf16),
-        pltpu.VMEM((2, width, 3 * GROUP), bf16), pltpu.VMEM((total, width), f32),
-        pltpu.SemaphoreType.DMA((5,)), pltpu.SemaphoreType.DMA((total // BLOCK,)),
+        pltpu.VMEM((total, 3 * width), bf16), pltpu.VMEM((total, width), bf16), pltpu.VMEM((total, width), bf16),
+        pltpu.VMEM((width, width), bf16), pltpu.VMEM((width, 3 * width), bf16), pltpu.VMEM((total, width), f32),
+        pltpu.SemaphoreType.DMA((6,)), pltpu.SemaphoreType.DMA((total // BLOCK,)),
     ]
     return pl.pallas_call(
         lambda *refs: backward_kernel(net, *refs),
@@ -1214,6 +1198,67 @@
     )(*operands)
 
 
+def unpack_kernel(
+    shard_ref, feed_ref, w_query_ref, w_key_ref, w_value_ref, gain_ref, result_in, grad_in,
+    query_ref, key_ref, value_ref, output_ref, expand_ref, reduce_ref, tile_ref, result_out, grad_out,
+    result_ref, grad_ref, sem,
+):
+    width = output_ref.shape[1]
+    parts = [
+        (source.at[pl.ds(r0, BLOCK)], held.at[pl.ds(r0, BLOCK)], target.at[pl.ds(r0, BLOCK)])
+        for r0 in range(0, result_ref.shape[0], BLOCK)
+        for source, held, target in ((result_in, result_ref, result_out), (grad_in, grad_ref, grad_out))
+    ]
+    loads = [pltpu.make_async_copy(source, held, sem.at[i]) for i, (source, held, _) in enumerate(parts)]
+    copies = [pltpu.make_async_copy(held, target, sem.at[i]) for i, (_, held, target) in enumerate(parts)]
+    begin(loads)
+    output_ref[...] = shard_ref[:, :width]
+    for k in range(expand_ref.shape[1] // GROUP):
+        cols = slice(k * GROUP, (k + 1) * GROUP)
+        expand_ref[:, cols] = feed_ref[:, 2 * k * GROUP : (2 * k + 1) * GROUP]
+        reduce_ref[:, cols] = feed_ref[:, (2 * k + 1) * GROUP : (2 * k + 2) * GROUP]
+    gain = 0.0
+    owned = (w_query_ref, w_key_ref, w_value_ref)
+    for j, (out, weight) in enumerate(zip((query_ref, key_ref, value_ref), owned)):
+        for p in range(width // LANES):
+            at = width + LANES + p * TRIO + j * LANES
+            out[:, p * LANES : (p + 1) * LANES] = shard_ref[:, at : at + LANES]
+        gain = gain + jnp.sum(weight[...].astype(f32) * out[...], axis=1, keepdims=True)
+    gain = gain / gain_ref[:, :1].astype(f32)
+    lane = lax.broadcasted_iota(jnp.int32, (1, LANES), 1)
+    tile = shard_ref[:, width : width + LANES]
+    means = jnp.sqrt(tile / (tile[:, 4:5] * width))
+    tile = jnp.where(lane == 5, gain, jnp.where(lane == 0, tile, means))
+    tile = jnp.concatenate([tile, jnp.zeros((LANES - tile.shape[0], LANES), f32)], axis=0)
+    tile_ref[...] = tile.T[:8]
+    for load, copy in zip(loads, copies):
+        load.wait()
+        copy.start()
+    for copy in copies:
+        copy.wait()
+
+
+def run_unpack(shard, shard_feed, weights, gain_tile, result, grad_tokens):
+    rows, width = weights[0].shape
+    rows_feed, both = shard_feed.shape
+    return pl.pallas_call(
+        unpack_kernel,
+        name="unpack_outputs",
+        out_shape=(
+            *(shape(rows, width, kind=f32) for _ in range(4)), shape(rows_feed, both // 2, kind=f32),
+            shape(rows_feed, both // 2, kind=f32), shape(8, LANES, kind=f32),
+            shape(*result.shape), shape(*grad_tokens.shape, kind=f32),
+        ),
+        in_specs=[VM] * 6 + [ANY] * 2,
+        out_specs=(VM,) * 7 + (ANY,) * 2,
+        scratch_shapes=[
+            pltpu.VMEM(result.shape, bf16), pltpu.VMEM(grad_tokens.shape, f32),
+            pltpu.SemaphoreType.DMA((2 * result.shape[0] // BLOCK,)),
+        ],
+        compiler_params=params(),
+    )(shard, shard_feed, *weights, gain_tile, result, grad_tokens)
+
+
 def on_device(
     net,
     tokens, clip_lengths, out_grad, w_query, w_key, w_value, w_output, gain_attention, gain_feed, w_expand, w_reduce,
@@ -1221,34 +1266,38 @@
     _, total, width = tokens.shape
     rows = tokens.reshape(total, width)
     out_grad = out_grad.reshape(total, width)
-    gain_tile = jnp.pad(jnp.stack([gain_attention, gain_feed], axis=1), ((0, 0), (0, LANES - 2)))
+    lane = lax.broadcasted_iota(jnp.int32, (1, LANES), 1)
+    gain_tile = jnp.where(lane == 0, gain_attention[:, None], jnp.where(lane == 1, gain_feed[:, None], 0))
     hid = w_expand.shape[1]
     if net is not None:
-        weights, _, qkv, mixed, lse, normed, feed_grads, result, grad_middle, sums, gains, *early = run_fused_forward(
-            net, clip_lengths, rows, out_grad, (w_query, w_key, w_value, w_output), gain_tile, w_expand, w_reduce
+        weights, _, qkv, mixed, extra, normed, feed_grads, result, grad_middle, sums, gains, *early = run_fused_forward(
+            net, clip_lengths, rows, out_grad, (w_query, w_key, w_value, w_output), gain_tile, w_expand, w_reduce.T
         )
         weights = weights.reshape(width, -1)
-        query, key, value, output, expand, reduce, tile, grad_tokens = run_backward(
-            net, clip_lengths, grad_middle, mixed, qkv, lse, normed, rows, weights, gains, sums, feed_grads,
-            w_query, w_key, w_value, gain_tile, *early,
+        shard, shard_feed, grad_tokens = run_backward(
+            net, clip_lengths, grad_middle, mixed, qkv, extra, normed, rows, weights, gains, sums, feed_grads, *early
         )
-        gain_one, gain_two, means = tile[:, LANES - 1], tile[:, 0], tile[0, 1:4]
+        query, key, value, output, expand, reduce, tile, result, grad_tokens = run_unpack(
+            shard, shard_feed, (w_query, w_key, w_value), gain_tile, result, grad_tokens
+        )
+        count = gain_feed.shape[0]
+        gain_one, gain_two, means, reduce = tile[5, :count], tile[0, :count], tile[1:4, 0], reduce.T
     else:
         mine = [w_output, gain_tile]
-        for g in range(width // GROUP):
-            mine += [w[:, g * GROUP : (g + 1) * GROUP] for w in (w_query, w_key, w_value)]
+        for p in range(width // LANES):
+            mine += [w[:, p * LANES : (p + 1) * LANES] for w in (w_query, w_key, w_value)]
         weights = lax.all_gather(jnp.concatenate(mine, axis=1), BOTH, axis=0, tiled=True)
         both = jnp.concatenate([w_expand, w_reduce.T], axis=1)
         feed_weights = lax.all_gather(both, BOTH[::-1], axis=0, tiled=True).reshape(-1, width, 2 * hid)
         gains = jnp.pad(weights[:, width : width + 2].T.astype(f32), ((0, 6), (0, 0)))
-        qkv, mixed, lse, middle, feed, normed, sums_one = run_forward(clip_lengths, rows, weights, gains)
+        qkv, mixed, extra, middle, feed, normed, sums_one = run_forward(clip_lengths, rows, weights, gains)
         feed_grads, result, grad_middle, sums_two = run_feed(
             clip_lengths, feed, out_grad, middle, gains, feed_weights
         )
         count = jnp.sum(clip_lengths[:, : SLOTS - 1]).astype(f32)
         squares = jnp.stack([jnp.sum(sums_one[0]), jnp.sum(sums_one[1]), jnp.sum(sums_two[0]), count])
         grads, grad_tokens = run_backward(
-            None, clip_lengths, grad_middle, mixed, qkv, lse, normed, rows, weights, gains
+            None, clip_lengths, grad_middle, mixed, qkv, extra, normed, rows, weights, gains
         )
         shard = lax.psum_scatter(grads, BOTH, scatter_dimension=0, tiled=True).astype(f32)
         shard_feed = lax.psum_scatter(
@@ -1257,7 +1306,7 @@
         stats = lax.psum(squares, BOTH)
         gain_two = lax.psum_scatter(sums_two[1], BOTH, scatter_dimension=0, tiled=True)
         means = jnp.sqrt(stats[:3] / (stats[3] * width))
-        parts = shard[:, width + LANES :].reshape(-1, width // GROUP, 3, GROUP)
+        parts = shard[:, width + LANES :].reshape(-1, width // LANES, 3, LANES)
         query, key, value = (parts[:, :, j].reshape(-1, width) for j in range(3))
         pairs = ((w_query, query), (w_key, key), (w_value, value))
         gain_one = sum(jnp.sum(w.astype(f32) * g, axis=1) for w, g in pairs) / gain_attention.astype(f32)

time: 223 us -> 210 us (0.942)
  local copies, waits for them, and re-layouts: 14.8 us -> 2.58 us
    unnamed x21 -> x0, local copies, waits for them, and re-layouts: 11.2 us -> none
    pallas_call x0 -> x1, Pallas kernels: none -> 6.24 us  [run_unpack(): pl.pallas_call(unpack_kernel, name='unpack_outputs', out_shape=(*(shape(r...]
    pallas_call x1, Pallas kernels: 125 us -> 119 us  [run_fused_forward(): pl.pallas_call(lambda *refs: fused_forward_kernel(net, *refs), name='laye...]
where the time goes in v1:
time: 210 us
  Pallas kernels  205 us (98%)
  local copies, waits for them, and re-layouts  2.58 us (1%)
    pallas_call x1, Pallas kernels, run_fused_forward(): pl.pallas_call(lambda *refs: fused_forward_kernel(net, *refs), name='laye...  119 us
    pallas_call x1, Pallas kernels, run_backward(): pl.pallas_call(lambda *refs: backward_kernel(net, *refs), name='layer_bac...  79.8 us
    pallas_call x1, Pallas kernels, run_unpack(): pl.pallas_call(unpack_kernel, name='unpack_outputs', out_shape=(*(shape(r...  6.24 us

profile of v1, /device:TPU:0, one launch (start us, length us, event | category | flops | bytes accessed | tf_op | source)
XLA Modules:
  0.0 209.9 jit_solution(14479749528586880805)
XLA Ops:
  0.7 1.3 select_select_fusion.refs_8_.gain_ref
  2.0 119.2 %layer_forward_feed.1 = (bf16[4,2,2,2,24,3200]{5,4,3,2,1,0:T(8,128)(2,1)}, bf16[2,2,4,2,96,1536]{5,4,3,2,1,0:T(8,128)(2,1)}, bf16[1024,2304]{1,0:T(8,128)(2,1)},...) custom-call(s32[1,4]{1,0:T(1,128)} %refs_0_.3, ...), custom_call_target="tpu_custom_call" | custom-call | tf_op jit(solution)/shard_map/layer_forward_feed/pallas_call | solution.py:1014
  121.3 79.8 %layer_backward.1 = (f32[24,3200]{1,0:T(8,128)}, f32[96,1536]{1,0:T(8,128)}, f32[1024,768]{1,0:T(8,128)}) custom-call(s32[1,4]{1,0:T(1,128)} %refs_0_.3, f32[1024,768]{1,0:T(8,128)} %get-tuple-element.37.refs_1_, bf16[1024,768]{1,0:T(8,128)(2,1)} %get-tuple-element.38.refs_2_, bf16[1024,2304]{1,0:T(8,128)(2,1)} %get-tuple-element.39.refs_3_, ...), custom_call_target="tpu_custom_call" | custom-call | flops 22000001024 | bytes 31457280 | tf_op jit(solution)/shard_map/layer_backward/pallas_call | solution.py:1189
  201.1 6.2 %unpack_outputs.1 = (f32[24,768]{1,0:T(8,128)}, f32[24,768]{1,0:T(8,128)}, f32[24,768]{1,0:T(8,128)}, f32[24,768]{1,0:T(8,128)}, f32[96,768]{1,0:T(8,128)}, /*in...) custom-call(f32[24,3200]{1,0:T(8,128)} %get-tuple-element.50.shard_ref, ...), custom_call_target="tpu_custom_call" | custom-call | tf_op jit(solution)/shard_map/unpack_outputs/pallas_call | solution.py:1244
  207.3 1.3 slice_reduce_fusion
  208.6 1.3 slice_bitcast_fusion
  (1 shorter events, 0.0 us)

commit v2 on v1

--- a/solution.py
+++ b/solution.py
@@ -318,13 +318,22 @@
 
 def backward_kernel(
     net,
-    clip_ref, grad_middle_ref, mixed_ref, qkv_hbm, extra_hbm, normed_hbm, tokens_hbm, weights_hbm, gains_ref,
+    clip_ref, grad_middle_hbm, mixed_hbm, qkv_hbm, extra_hbm, normed_hbm, tokens_hbm, weights_hbm, gains_ref,
     *refs,
 ):
-    total, width = mixed_ref.shape
+    total, width = mixed_hbm.shape
     ends = clip_ends(clip_ref)
     refs, load_sem, store_sem = refs[:-2], *refs[-2:]
     refs, (qkv_ref, extra_ref, normed_ref, output_weight_ref, weight_ref, sum_ref) = refs[:-6], refs[-6:]
+    refs, (grad_middle_ref, mixed_ref) = refs[:-2], refs[-2:]
+    if net is not None:
+        net.locate()
+        net.announce()
+    firsts = [
+        pltpu.make_async_copy(grad_middle_hbm, grad_middle_ref, load_sem.at[6]),
+        pltpu.make_async_copy(mixed_hbm, mixed_ref, load_sem.at[7]),
+    ]
+    begin(firsts)
     pairs = width // LANES
     loads = [
         pltpu.make_async_copy(source, target, load_sem.at[i])
@@ -338,8 +347,8 @@
             )
         )
     ]
-    begin(loads)
     if net is None:
+        begin(loads)
         grads_ref, grad_tokens_ref, low_ref, grad_ref, dqkv_ref, dq_ref, inner_ref, code_k_ref = refs
         plan = {}
     else:
@@ -347,9 +356,14 @@
         early, refs = refs[: 2 * EARLY], refs[2 * EARLY :]
         shard_ref, shard_feed_ref, grad_tokens_ref, low_ref, grad_ref, dqkv_ref, dq_ref, inner_ref, *refs = refs
         code_k_ref, grads_ref, own_ref, send, recv, local, *bufs = refs
-        net.locate()
-        net.announce()
-        net.meet()
+        held, bufs = bufs[: 2 * EARLY], bufs[2 * EARLY :]
+        halves_in = [
+            pltpu.make_async_copy(source, target, load_sem.at[8 + i])
+            for i, (source, target) in enumerate(zip(early, held))
+        ]
+        begin(halves_in)
+        begin(loads)
+        early = held
         sems = Sems(send, recv)
         feed, att = [], []
         flip = BOTH[::-1]
@@ -372,8 +386,11 @@
             att.append(Fold(net, sems, grads_ref, BOTH, lanes, along, bufs[:4], shard_ref))
             bufs = bufs[4:]
         early, late = feed[: 2 * EARLY], feed[2 * EARLY :]
+        net.meet()
         for p in late:
             p.send(0)
+        for copy in halves_in:
+            copy.wait()
         for p in early:
             p.send(2)
         mine = tuple(net.place["c"] if n == "c" else slice(None) for n in net.names(flip))
@@ -404,6 +421,8 @@
 
     if net is not None:
         store(slice(width, width + LANES), extras)
+    for copy in firsts:
+        copy.wait()
     low_ref[...] = grad_middle_ref[...].astype(bf16)
     store(slice(0, width), dot_first(mixed_ref[...], low_ref[...]))
     if net is not None:
@@ -634,7 +653,7 @@
 
 
 class Piece:
-    def __init__(self, net, sems, mine, ref, order, lanes, first, second):
+    def __init__(self, net, sems, mine, ref, order, lanes, first, second, third):
         def block(free, **other):
             fixed = {n: v for n, v in net.place.items() if n not in free}
             return net.view(ref, order, lanes, **{**fixed, **other})
@@ -643,13 +662,13 @@
             return spread(net, sems, dim, part, part)
 
         self.left = False
-        self.z = spread(net, sems, "z", mine.at[:, pl.ds(*lanes)], block(()))
-        self.one = pass_on(first, block(("z",)))
-        self.two = pass_on(second, block(("z", first)))
+        self.z = spread(net, sems, first, mine.at[:, pl.ds(*lanes)], block(()))
+        self.one = pass_on(second, block((first,)))
+        self.two = pass_on(third, block((first, second)))
         self.twins = [
-            pass_on("c", block(("z",))),
-            sum((pass_on("c", block(("z",), **{first: v})) for v in net.peers(first)), []),
-            sum((pass_on("c", block(("z", first), **{second: v})) for v in net.peers(second)), []),
+            pass_on("c", block((first,))),
+            sum((pass_on("c", block((first,), **{second: v})) for v in net.peers(second)), []),
+            sum((pass_on("c", block((first, second), **{third: v})) for v in net.peers(third)), []),
         ]
 
     def start(self):
@@ -682,7 +701,7 @@
 
 def copies_of(net):
     z, y, x, c = (net.size[n] - 1 for n in "zyxc")
-    return z + y + x + c * (1 + y + x)
+    return z + y + x + c * (1 + z + y + x)
 
 
 def lane_parts(width, count):
@@ -694,7 +713,8 @@
     return out
 
 
-ORDERS = (("y", "x"), ("x", "y"))
+ORDERS = (("z", "y", "x"), ("z", "x", "y"))
+ORDERS_LATE = (("y", "z", "x"), ("x", "z", "y"))
 
 
 def att_spans(width):
@@ -747,7 +767,7 @@
     ]
     feed = [
         [
-            Piece(net, sems, both_ref, feed_all, flip, lanes, *ORDERS[i])
+            Piece(net, sems, both_ref, feed_all, flip, lanes, *(ORDERS_LATE if k >= LATE else ORDERS)[i])
             for i, lanes in enumerate(halves(2 * k * GROUP, 2 * GROUP))
         ]
         for k in range(chunks)
@@ -822,8 +842,8 @@
         1: [("step_two", pair[5]), ("step_three", pair[3]), ("start", output)],
         2: [("start", feed[1]), ("step_three", pair[4]), ("ready", pair[2])],
         3: [("step_one", feed[0]), ("step_three", pair[5])],
-        4: [("step_one", output), ("ready", pair[3])],
-        6: [("step_two", output), ("step_two", feed[0]), ("start", feed[2]), ("ready", pair[4])],
+        4: [("start", feed[2]), ("step_one", output), ("ready", pair[3])],
+        6: [("step_one", feed[2]), ("step_two", output), ("step_two", feed[0]), ("ready", pair[4])],
         8: [("step_one", feed[1]), ("ready", pair[5])],
         9: [("step_three", output)],
         11: [("step_three", feed[0])],
@@ -863,7 +883,7 @@
         copy.start()
     fetch((0, width), output_weight_ref, local.at[1]).wait()
     middle_ref[...] = dot_plain(mixed_ref[...], flat(output_weight_ref[...]))
-    act(("step_two", feed[1]), ("step_one", feed[2]))
+    act(("step_two", feed[1]))
 
     def second(r0):
         rows = pl.ds(r0, BLOCK)
@@ -875,7 +895,7 @@
 
     row_loop(total, BLOCK, second)
     act(("ready", feed[0]))
-    feed_plan = {(0, 3): [("step_three", feed[1]), ("step_two", feed[2])], (1, 3): [("step_three", feed[2])]}
+    feed_plan = {(0, 2): [("step_three", feed[1]), ("step_two", feed[2])], (1, 2): [("step_three", feed[2])]}
 
     tp = net.names(("tp",))
     quarters = list(np.ndindex(*(net.size[n] for n in tp)))
@@ -1138,6 +1158,7 @@
 
 
 EARLY = 2
+LATE = 2
 
 
 def att_folds(width):
@@ -1157,7 +1178,7 @@
         pltpu.VMEM((total, LANES), f32), pltpu.VMEM((total, width), bf16), pltpu.VMEM((total, LANES), bf16),
     ]
     operands = [clip, grad_middle, mixed, qkv, extra, normed, tokens, weights, gains]
-    in_specs = [SM, VM, VM, ANY, ANY, ANY, ANY, ANY, VM]
+    in_specs = [SM] + [ANY] * 7 + [VM]
     out_shape = (shape(width, lanes), shape(total, width, kind=f32))
     more = {}
     if net is not None:
@@ -1166,7 +1187,7 @@
         hid = feed_grads.shape[-1] // 2
         flip = BOTH[::-1]
         operands += more_args
-        in_specs += [VM, ANY] + [VM] * (2 * EARLY)
+        in_specs += [VM, ANY] + [ANY] * (2 * EARLY)
         out_shape = (shape(rows, lanes, kind=f32), shape(rows_feed, 2 * hid, kind=f32), out_shape[1])
         scratch.append(pltpu.VMEM((*net.dims(BOTH), rows, lanes), bf16))
         kept = tuple(net.size[n] for n in net.names(flip) if n != "c")
@@ -1179,12 +1200,14 @@
             bufs += Fold.shapes(net, BOTH, rows, *f)
         count = sum(dims[0] for dims in bufs)
         scratch += [pltpu.SemaphoreType.DMA((count,)), pltpu.SemaphoreType.DMA((count,)), pltpu.SemaphoreType.DMA]
+        scratch += [pltpu.VMEM(half.shape, bf16) for half in more_args[2:]]
         scratch += [pltpu.VMEM(dims, bf16) for dims in bufs]
         more = dict(collective_id=2, has_side_effects=True)
     scratch += [
+        pltpu.VMEM((total, width), f32), pltpu.VMEM((total, width), bf16),
         pltpu.VMEM((total, 3 * width), bf16), pltpu.VMEM((total, width), bf16), pltpu.VMEM((total, width), bf16),
         pltpu.VMEM((width, width), bf16), pltpu.VMEM((width, 3 * width), bf16), pltpu.VMEM((total, width), f32),
-        pltpu.SemaphoreType.DMA((6,)), pltpu.SemaphoreType.DMA((total // BLOCK,)),
+        pltpu.SemaphoreType.DMA((8 + 2 * EARLY,)), pltpu.SemaphoreType.DMA((total // BLOCK,)),
     ]
     return pl.pallas_call(
         lambda *refs: backward_kernel(net, *refs),
@@ -1200,8 +1223,8 @@
 
 def unpack_kernel(
     shard_ref, feed_ref, w_query_ref, w_key_ref, w_value_ref, gain_ref, result_in, grad_in,
-    query_ref, key_ref, value_ref, output_ref, expand_ref, reduce_ref, tile_ref, result_out, grad_out,
-    result_ref, grad_ref, sem,
+    query_ref, key_ref, value_ref, output_ref, expand_ref, reduce_ref, gain_one_ref, gain_two_ref, means_ref,
+    result_out, grad_out, result_ref, grad_ref, sem,
 ):
     width = output_ref.shape[1]
     parts = [
@@ -1230,7 +1253,12 @@
     means = jnp.sqrt(tile / (tile[:, 4:5] * width))
     tile = jnp.where(lane == 5, gain, jnp.where(lane == 0, tile, means))
     tile = jnp.concatenate([tile, jnp.zeros((LANES - tile.shape[0], LANES), f32)], axis=0)
-    tile_ref[...] = tile.T[:8]
+    rows = tile.T
+    count = gain_one_ref.shape[0]
+    gain_one_ref[...] = rows[5, :count]
+    gain_two_ref[...] = rows[0, :count]
+    lane = lax.broadcasted_iota(jnp.int32, (1, LANES), 1)
+    means_ref[...] = jnp.where(lane == 0, rows[1:2], jnp.where(lane == 1, rows[2:3], rows[3:4]))[0, :3]
     for load, copy in zip(loads, copies):
         load.wait()
         copy.start()
@@ -1246,11 +1274,11 @@
         name="unpack_outputs",
         out_shape=(
             *(shape(rows, width, kind=f32) for _ in range(4)), shape(rows_feed, both // 2, kind=f32),
-            shape(rows_feed, both // 2, kind=f32), shape(8, LANES, kind=f32),
+            shape(rows_feed, both // 2, kind=f32), shape(rows, kind=f32), shape(rows, kind=f32), shape(3, kind=f32),
             shape(*result.shape), shape(*grad_tokens.shape, kind=f32),
         ),
         in_specs=[VM] * 6 + [ANY] * 2,
-        out_specs=(VM,) * 7 + (ANY,) * 2,
+        out_specs=(VM,) * 9 + (ANY,) * 2,
         scratch_shapes=[
             pltpu.VMEM(result.shape, bf16), pltpu.VMEM(grad_tokens.shape, f32),
             pltpu.SemaphoreType.DMA((2 * result.shape[0] // BLOCK,)),
@@ -1277,11 +1305,10 @@
         shard, shard_feed, grad_tokens = run_backward(
             net, clip_lengths, grad_middle, mixed, qkv, extra, normed, rows, weights, gains, sums, feed_grads, *early
         )
-        query, key, value, output, expand, reduce, tile, result, grad_tokens = run_unpack(
+        query, key, value, output, expand, reduce, gain_one, gain_two, means, result, grad_tokens = run_unpack(
             shard, shard_feed, (w_query, w_key, w_value), gain_tile, result, grad_tokens
         )
-        count = gain_feed.shape[0]
-        gain_one, gain_two, means, reduce = tile[5, :count], tile[0, :count], tile[1:4, 0], reduce.T
+        reduce = reduce.T
     else:
         mine = [w_output, gain_tile]
         for p in range(width // LANES):

time: 210 us -> 203 us (0.967)
  Pallas kernels: 205 us -> 201 us
  local copies, waits for them, and re-layouts: 2.58 us -> 0 us
    pallas_call x1, Pallas kernels: 119 us -> 117 us  [run_fused_forward(): pl.pallas_call(lambda *refs: fused_forward_kernel(net, *refs), name='laye...]
where the time goes in v2:
time: 203 us
  Pallas kernels  201 us (99%)
    pallas_call x1, Pallas kernels, run_fused_forward(): pl.pallas_call(lambda *refs: fused_forward_kernel(net, *refs), name='laye...  117 us
    pallas_call x1, Pallas kernels, run_backward(): pl.pallas_call(lambda *refs: backward_kernel(net, *refs), name='layer_bac...  78 us
    pallas_call x1, Pallas kernels, run_unpack(): pl.pallas_call(unpack_kernel, name='unpack_outputs', out_shape=(*(shape(r...  6.24 us

profile of v2, /device:TPU:0, one launch (start us, length us, event | category | flops | bytes accessed | tf_op | source)
XLA Modules:
  0.0 203.0 jit_solution(13481208832232869559)
XLA Ops:
  0.7 1.3 select_select_fusion.refs_8_.gain_ref
  2.0 116.6 %layer_forward_feed.1 = (bf16[4,2,2,2,24,3200]{5,4,3,2,1,0:T(8,128)(2,1)}, bf16[2,2,4,2,96,1536]{5,4,3,2,1,0:T(8,128)(2,1)}, bf16[1024,2304]{1,0:T(8,128)(2,1)},...) custom-call(s32[1,4]{1,0:T(1,128)} %refs_0_.3, ...), custom_call_target="tpu_custom_call" | custom-call | tf_op jit(solution)/shard_map/layer_forward_feed/pallas_call | solution.py:1034
  118.6 78.0 %layer_backward.1 = (f32[24,3200]{1,0:T(8,128)}, f32[96,1536]{1,0:T(8,128)}, f32[1024,768]{1,0:T(8,128)}) custom-call(s32[1,4]{1,0:T(1,128)} %refs_0_.3, f32[1024,768]{1,0:T(8,128)} %get-tuple-element.39.refs_1_, bf16[1024,768]{1,0:T(8,128)(2,1)} %get-tuple-element.40.refs_2_, bf16[1024,2304]{1,0:T(8,128)(2,1)} %get-tuple-element.41.refs_3_, ...), custom_call_target="tpu_custom_call" | custom-call | flops 22000001024 | bytes 31457280 | tf_op jit(solution)/shard_map/layer_backward/pallas_call | solution.py:1212
  196.6 6.2 %unpack_outputs.1 = (f32[24,768]{1,0:T(8,128)}, f32[24,768]{1,0:T(8,128)}, f32[24,768]{1,0:T(8,128)}, f32[24,768]{1,0:T(8,128)}, f32[96,768]{1,0:T(8,128)}, /*in...) custom-call(f32[24,3200]{1,0:T(8,128)} %get-tuple-element.52.shard_r, ...), custom_call_target="tpu_custom_call" | custom-call | tf_op jit(solution)/shard_map/unpack_outputs/pallas_call | solution.py:1272
  (1 shorter events, 0.0 us)

commit v3 on v2

--- a/solution.py
+++ b/solution.py
@@ -450,15 +450,13 @@
             7: [(pair[2], 0), (pair[1], 1), (late, 2), (pair[0], 2)],
             8: [(early, 3)],
             9: [(pair[3], 0), (pair[2], 1), (pair[1], 2)],
-            10: [(output, 3), (pair[0], 3)],
-            11: [(pair[4], 0), (pair[3], 1), (pair[2], 2), (late, 3)],
+            11: [(pair[4], 0), (pair[3], 1), (pair[2], 2)],
         }
         ending = {
-            0: [(pair[4], 1), (pair[3], 2), (pair[1], 3)],
+            0: [(pair[4], 1), (pair[3], 2)],
             1: [(pair[5], 0)],
-            2: [(pair[2], 3)],
             4: [(pair[4], 2)],
-            6: [(pair[5], 1), (pair[3], 3)],
+            5: [(pair[5], 1)],
         }
     for copy in loads[1:]:
         copy.wait()
@@ -508,8 +506,8 @@
         finals[-1].start()
         advance(*ending.get(3 + b, ()))
     if net is not None:
-        advance((pair[5], 2), (pair[4], 3))
-        advance((pair[5], 3))
+        advance((output, 3), (pair[0], 3), (pair[1], 3))
+        advance((pair[5], 2), (late, 3), (pair[2], 3), (pair[3], 3), (pair[4], 3), (pair[5], 3))
         for p in feed + att:
             p.drain()
     for copy in finals:

time: 203 us -> 201 us (level)
    pallas_call x1, Pallas kernels: 78 us -> 75.9 us  [run_backward(): pl.pallas_call(lambda *refs: backward_kernel(net, *refs), name='layer_bac...]
where the time goes in v3:
time: 201 us
  Pallas kernels  199 us (99%)
    pallas_call x1, Pallas kernels, run_fused_forward(): pl.pallas_call(lambda *refs: fused_forward_kernel(net, *refs), name='laye...  117 us
    pallas_call x1, Pallas kernels, run_backward(): pl.pallas_call(lambda *refs: backward_kernel(net, *refs), name='layer_bac...  75.9 us
    pallas_call x1, Pallas kernels, run_unpack(): pl.pallas_call(unpack_kernel, name='unpack_outputs', out_shape=(*(shape(r...  6.24 us

profile of v3, /device:TPU:0, one launch (start us, length us, event | category | flops | bytes accessed | tf_op | source)
XLA Modules:
  0.0 201.0 jit_solution(11492580284965840515)
XLA Ops:
  0.7 1.3 select_select_fusion.refs_8_.gain_ref
  2.0 116.6 %layer_forward_feed.1 = (bf16[4,2,2,2,24,3200]{5,4,3,2,1,0:T(8,128)(2,1)}, bf16[2,2,4,2,96,1536]{5,4,3,2,1,0:T(8,128)(2,1)}, bf16[1024,2304]{1,0:T(8,128)(2,1)},...) custom-call(s32[1,4]{1,0:T(1,128)} %refs_0_.3, ...), custom_call_target="tpu_custom_call" | custom-call | tf_op jit(solution)/shard_map/layer_forward_feed/pallas_call | solution.py:1032
  118.6 75.9 %layer_backward.1 = (f32[24,3200]{1,0:T(8,128)}, f32[96,1536]{1,0:T(8,128)}, f32[1024,768]{1,0:T(8,128)}) custom-call(s32[1,4]{1,0:T(1,128)} %refs_0_.3, f32[1024,768]{1,0:T(8,128)} %get-tuple-element.39.refs_1_, bf16[1024,768]{1,0:T(8,128)(2,1)} %get-tuple-element.40.refs_2_, bf16[1024,2304]{1,0:T(8,128)(2,1)} %get-tuple-element.41.refs_3_, ...), custom_call_target="tpu_custom_call" | custom-call | flops 22000001024 | bytes 31457280 | tf_op jit(solution)/shard_map/layer_backward/pallas_call | solution.py:1210
  194.5 6.2 %unpack_outputs.1 = (f32[24,768]{1,0:T(8,128)}, f32[24,768]{1,0:T(8,128)}, f32[24,768]{1,0:T(8,128)}, f32[24,768]{1,0:T(8,128)}, f32[96,768]{1,0:T(8,128)}, /*in...) custom-call(f32[24,3200]{1,0:T(8,128)} %get-tuple-element.52.shard_r, ...), custom_call_target="tpu_custom_call" | custom-call | tf_op jit(solution)/shard_map/unpack_outputs/pallas_call | solution.py:1270
  (1 shorter events, 0.0 us)
